TPU v7x, 256 devices: a whole 4x4x8 slice. The times are simulated.
256 devices in a mesh: ctx: 32 (over y_lo, z, core), head: 8 (over y_hi, x).
Axes of the slice: x: 4, y: 4 (y_hi: 2, y_lo: 2; y = y_hi * 2 + y_lo), z: 8, core: 2. Of those that a mesh axis runs over, the one named last changes fastest.
Arguments:
- fine_query: bfloat16 [8192, 4096], P('ctx', 'head'), may hold values from -181 to 181
- fine_memory: bfloat16 [2, 8192, 1024], P(None, 'ctx', 'head'), may hold values from -6.5 to 6.5
- coarse_query: bfloat16 [4096, 4096], P('ctx', 'head'), may hold values from -181 to 181
- coarse_memory: bfloat16 [2, 4096, 1024], P(None, 'ctx', 'head'), may hold values from -6.5 to 6.5
- coarse_scale: int32 [4096], P('ctx'), may hold values from 0 to 7, never falling along the last dimension, each value on 1 to 1024 neighbouring positions
- out_weight: bfloat16 [4096, 4096], P('head'), may hold values from -0.09375 to 0.09375
Outputs:
- fine_mixed: bfloat16 [8192, 4096], P(('ctx', 'head'))
- coarse_mixed: bfloat16 [4096, 4096], P(('ctx', 'head'))
Inputs may be any that keep to these rules, and one draw needn't show every extreme that they name: `coarse_scale`: never falls along the coarse tokens.
All inputs are finite; a program needn't handle non-finite values.
Results may differ from a plain program's by a relative error of at most 0.014.
Values may be sent and summed in bfloat16 or wider, within the bound.
No kernel may reach another device: no remote copies, remote signals or barrier semaphores. Data moves between devices by JAX's collectives and lax.ppermute only.
A program may use at most 64 MiB of HBM per device.

v0:
```python
import functools
import math

import jax
import jax.numpy as jnp
from jax import lax
from jax.experimental import pallas as pl
from jax.experimental.pallas import tpu as pltpu
from jax.sharding import Mesh
from jax.sharding import PartitionSpec as P

HD = 128
PAD = 16
CTX = ("yl", "z", "c")
HEAD = ("yh", "xp", "xl")
LOW = -1e30
EXPONENT = HD**-0.5 * math.log2(math.e)
NT = (((1,), (1,)), ((), ()))
NN = (((1,), (0,)), ((), ()))
GRANT = 24 << 20
TILE = 256


def dot_nt(a, b):
    return lax.dot_general(a, b, NT, preferred_element_type=jnp.float32)


def dot_nn(a, b):
    return lax.dot_general(a, b, NN, preferred_element_type=jnp.float32)


def whole(shape):
    return pl.BlockSpec(shape, lambda *_: (0,) * len(shape))


def rows_of(ref, start, length):
    return ref[:, start : start + length, :].reshape(-1, HD)


def in_three(x, which):
    result = jnp.zeros_like(x)
    for i in range(3):
        part = x.astype(jnp.bfloat16).astype(jnp.float32)
        result = jnp.where(which == i, part, result)
        x = x - part
    return result.astype(jnp.bfloat16)


def fold_kernel(n_blocks, fine, coarse, first, last, tile, q_ref, cq_ref, level_ref, *refs):
    blocks, refs = refs[:n_blocks], refs[n_blocks:]
    if not first:
        state, refs = refs[:4], refs[4:]
    heads = q_ref.shape[1] // HD
    at = 2 * fine
    k_fine = [rows_of(b, 0, fine) for b in blocks]
    v_fine = [rows_of(b, fine, fine) for b in blocks]
    k_coarse = [rows_of(b, at, coarse) for b in blocks]
    v_coarse = [rows_of(b, at + coarse, coarse) for b in blocks]
    at = at + 2 * coarse
    key_level = jnp.concatenate(
        [b[i, at : at + 1, :] for b in blocks for i in range(b.shape[0])], axis=1
    ).astype(jnp.float32)
    k = jnp.concatenate(k_fine + k_coarse, axis=0)
    v = jnp.concatenate(v_fine + v_coarse, axis=0)
    v = jnp.concatenate([v, jnp.ones_like(v)], axis=1)
    n_fine = k.shape[0] - key_level.shape[1]

    def attend(queries, keys, values, allowed, h, rows, m_in, acc_in, m_out, acc_out):
        s = dot_nt(queries[rows, h * HD : (h + 1) * HD], keys)
        if allowed is not None:
            s = jnp.where(allowed, s, LOW)
        top = jnp.max(s, axis=1, keepdims=True)
        if first:
            new = jnp.broadcast_to(top, (tile, HD))
        else:
            old = m_in[h, rows, :]
            new = jnp.maximum(old, top)
        p = jnp.exp2(s * EXPONENT - new[:, :1] * EXPONENT).astype(jnp.bfloat16)
        acc = dot_nn(p, values)
        if not first:
            acc = acc + acc_in[h, rows, :] * jnp.exp2((old - new) * EXPONENT)[:, :1]
        if not last:
            m_out[h, rows, :] = new
            acc_out[h, rows, :] = acc
            return None
        return (acc[:, :HD] / acc[:, HD:]).astype(jnp.bfloat16), new, acc[:, HD:]

    lane = lax.broadcasted_iota(jnp.int32, (tile, HD), 1)
    for is_coarse in (False, True):
        queries = cq_ref if is_coarse else q_ref
        pair = 2 if is_coarse else 0
        m_in, acc_in = (None, None) if first else state[pair : pair + 2]
        m_out, acc_out = (None, None) if last else refs[pair : pair + 2]
        for t in range(queries.shape[0] // tile):
            rows = slice(t * tile, (t + 1) * tile)
            if is_coarse:
                allowed = key_level <= level_ref[rows, :1]
                keys, values = k[n_fine:], v[n_fine:]
            else:
                allowed, keys, values = None, k, v
            top = jnp.zeros((tile, HD), jnp.float32)
            total = jnp.ones((tile, HD), jnp.float32)
            for h in range(heads):
                done = attend(queries, keys, values, allowed, h, rows, m_in, acc_in, m_out, acc_out)
                if last:
                    place(refs, is_coarse, t, tile, q_ref.shape[0] // 4, h, done[0])
                    top = jnp.where(lane // 3 == h, done[1], top)
                    total = jnp.where(lane // 3 == h, done[2], total)
            if last:
                stats = in_three(top * EXPONENT + jnp.log(total) * math.log2(math.e), lane % 3)
                place(refs, is_coarse, t, tile, q_ref.shape[0] // 4, heads, stats)


def place(outs, is_coarse, t, tile, n_fine, h, value):
    n = outs[0].shape[0] - n_fine if is_coarse else n_fine
    for i in range(max(1, tile // n)):
        row = t * tile + i * n
        start = row % n + (n_fine if is_coarse else 0)
        length = min(n, tile)
        outs[row // n][start : start + length, h * HD : (h + 1) * HD] = value[
            i * n : i * n + length
        ]


def fold(q, cq, level, blocks, state, last, fine, coarse):
    heads = q.shape[1] // HD
    first = state is None
    ins = (q, cq, level, *blocks, *(() if first else state))
    if last:
        quarter = (q.shape[0] + cq.shape[0]) // 4
        out = (jax.ShapeDtypeStruct((quarter, q.shape[1] + HD), jnp.bfloat16),) * 4
    else:
        out = tuple(
            jax.ShapeDtypeStruct((heads, rows, width), jnp.float32)
            for rows in (q.shape[0], cq.shape[0])
            for width in (HD, 2 * HD)
        )
    work = heads * sum(b.shape[0] for b in blocks) * (q.shape[0] * (fine + coarse) + cq.shape[0] * coarse)
    aliases = {} if first or last else {len(ins) - 4 + i: i for i in range(4)}
    return pl.pallas_call(
        functools.partial(fold_kernel, len(blocks), fine, coarse, first, last, TILE),
        out_shape=out,
        in_specs=[whole(a.shape) for a in ins],
        out_specs=tuple(whole(o.shape) for o in out),
        input_output_aliases=aliases,
        compiler_params=pltpu.CompilerParams(vmem_limit_bytes=GRANT),
        cost_estimate=pl.CostEstimate(
            flops=work, bytes_accessed=q.size, transcendentals=0
        ),
        name="fold",
    )(*ins)


def project_kernel(n_fine, n_blocks, core_ref, keep, near, cross, far, w, w_mine, w_other, o_ref, a_ref):
    heads = keep.shape[1] // HD - 1
    rows = keep.shape[0]
    width = heads * HD
    half = width // 2

    @pl.when(pl.program_id(0) == 0)
    def _():
        swap = jnp.broadcast_to(core_ref[0], (1, 1)) == 1
        for g, (one, two) in enumerate(((keep, near), (cross, far))):
            merged = []
            for h in range(heads):
                stat = []
                for ref in (one, two):
                    s = ref[:, width:].astype(jnp.float32)
                    stat.append(s[:, 3 * h : 3 * h + 1] + s[:, 3 * h + 1 : 3 * h + 2] + s[:, 3 * h + 2 : 3 * h + 3])
                top = jnp.maximum(stat[0], stat[1])
                w0, w1 = jnp.exp2(stat[0] - top), jnp.exp2(stat[1] - top)
                cols = slice(h * HD, (h + 1) * HD)
                total = one[:, cols].astype(jnp.float32) * w0 + two[:, cols].astype(jnp.float32) * w1
                merged.append((total / (w0 + w1)).astype(jnp.bfloat16))
            merged = jnp.concatenate(merged, axis=1)
            if g == 1:
                lower, upper = merged[:, :half], merged[:, half:]
                merged = jnp.concatenate(
                    [jnp.where(swap, upper, lower), jnp.where(swap, lower, upper)], axis=1
                )
            n_coarse = rows - n_fine
            f, c = n_fine // n_blocks, n_coarse // n_blocks
            for b in range(n_blocks):
                at = b * (f + c)
                cols = slice(g * width, (g + 1) * width)
                a_ref[at : at + f, cols] = merged[b * f : (b + 1) * f]
                a_ref[at + f : at + f + c, cols] = merged[n_fine + b * c : n_fine + (b + 1) * c]

    o_ref[...] = (
        dot_nn(a_ref[:, :width], w[...])
        + dot_nn(a_ref[:, width : width + half], w_mine[...])
        + dot_nn(a_ref[:, width + half :], w_other[...])
    ).astype(jnp.bfloat16)


def project(core, parts, weights, n_fine, n_blocks):
    rows = parts[0].shape[0]
    columns = weights[0].shape[1]
    tile = math.gcd(columns, 1024)
    depth = sum(w.shape[0] for w in weights)
    return pl.pallas_call(
        functools.partial(project_kernel, n_fine, n_blocks),
        grid=(columns // tile,),
        out_shape=jax.ShapeDtypeStruct((rows, columns), jnp.bfloat16),
        in_specs=[pl.BlockSpec(memory_space=pltpu.SMEM)]
        + [whole(p.shape) for p in parts]
        + [pl.BlockSpec((w.shape[0], tile), lambda j: (0, j)) for w in weights],
        out_specs=pl.BlockSpec((rows, tile), lambda j: (0, j)),
        scratch_shapes=[pltpu.VMEM((rows, depth), jnp.bfloat16)],
        compiler_params=pltpu.CompilerParams(vmem_limit_bytes=GRANT),
        cost_estimate=pl.CostEstimate(
            flops=2 * rows * depth * columns, bytes_accessed=2 * depth * columns, transcendentals=0
        ),
        name="project",
    )(core, *parts, *weights)


def crossed(x, axes):
    n = 2 ** len(axes)
    return lax.ppermute(x, axes, [(i, n - 1 - i) for i in range(n)])


def along_z(x, hops):
    n = lax.axis_size("z")
    pairs = []
    for z in range(n):
        pairs.append((2 * z, 2 * ((z + hops) % n)))
        pairs.append((2 * z + 1, 2 * ((z - hops) % n) + 1))
    return lax.ppermute(x, ("z", "c"), pairs)


def arrange_kernel(n_yh, n_xp, n_xl, xp_ref, fine_mine, fine_theirs, coarse_mine, coarse_theirs, q, cq, level):
    n = n_yh * n_xl
    width = q.shape[1]
    for whose, (fine, coarse) in enumerate(((fine_mine, coarse_mine), (fine_theirs, coarse_theirs))):
        for part in range(2):
            xp = xp_ref[0] if part == 0 else 1 - xp_ref[0]
            for i in range(n):
                block = (i // n_xl * n_xp + xp) * n_xl + i % n_xl
                at = (whose * 2 + part) * n + i
                size = fine.shape[0] // (2 * n)
                start = pl.multiple_of(block * size, size)
                q[at * size : (at + 1) * size, :] = fine[pl.ds(start, size), :]
                size = coarse.shape[0] // (2 * n)
                start = pl.multiple_of(block * size, size)
                rows = coarse[pl.ds(start, size), :]
                cq[at * size : (at + 1) * size, :] = rows[:, :width]
                level[at * size : (at + 1) * size, :] = rows[:, width:].astype(jnp.float32)


def arranged(xp, arrays):
    fine, coarse = arrays[0], arrays[2]
    width = fine.shape[1]
    out = (
        jax.ShapeDtypeStruct((2 * fine.shape[0], width), jnp.bfloat16),
        jax.ShapeDtypeStruct((2 * coarse.shape[0], width), jnp.bfloat16),
        jax.ShapeDtypeStruct((2 * coarse.shape[0], HD), jnp.float32),
    )
    return pl.pallas_call(
        functools.partial(arrange_kernel, *(lax.axis_size(a) for a in HEAD)),
        out_shape=out,
        in_specs=[pl.BlockSpec(memory_space=pltpu.SMEM)] + [whole(a.shape) for a in arrays],
        out_specs=tuple(whole(o.shape) for o in out),
        compiler_params=pltpu.CompilerParams(vmem_limit_bytes=GRANT),
        cost_estimate=pl.CostEstimate(
            flops=0, bytes_accessed=sum(4 * a.size for a in arrays), transcendentals=0
        ),
        name="arrange",
    )(xp, *arrays)


def total_kernel(got, first, second):
    n = first.shape[0]
    total = got[0].astype(jnp.float32)
    for i in range(1, got.shape[0]):
        total = total + got[i].astype(jnp.float32)
    first[...] = total[:n].astype(jnp.bfloat16)
    second[...] = total[n:].astype(jnp.bfloat16)


def totals(got, n):
    parts, rows, columns = got.shape
    tile = math.gcd(columns, 1024)
    return pl.pallas_call(
        functools.partial(total_kernel),
        grid=(columns // tile,),
        out_shape=tuple(
            jax.ShapeDtypeStruct((r, columns), jnp.bfloat16) for r in (n, rows - n)
        ),
        in_specs=[pl.BlockSpec((parts, rows, tile), lambda j: (0, 0, j))],
        out_specs=tuple(pl.BlockSpec((r, tile), lambda j: (0, j)) for r in (n, rows - n)),
        cost_estimate=pl.CostEstimate(flops=got.size, bytes_accessed=3 * got.size, transcendentals=0),
        name="totals",
    )(got)


def per_device(fine_query, fine_memory, coarse_query, coarse_memory, coarse_scale, out_weight):
    fine, coarse = fine_query.shape[0], coarse_query.shape[0]
    width = fine_query.shape[1]
    levels = coarse_scale.astype(jnp.bfloat16)
    level_rows = jnp.broadcast_to(levels[None, :], (PAD, HD))
    piece = jnp.concatenate(
        [fine_memory.reshape(-1, HD), coarse_memory.reshape(-1, HD), level_rows], axis=0
    )
    coarse_mine = jnp.concatenate(
        [coarse_query, jnp.broadcast_to(levels[:, None], (coarse, HD))], axis=1
    )
    fine_theirs = crossed(fine_query, ("yl",))
    coarse_theirs = crossed(coarse_mine, ("yl",))

    chip = jnp.stack([piece, crossed(piece, ("c",))])
    one, two = along_z(chip, 1), along_z(chip, 2)

    core = lax.axis_index("c")
    depth = out_weight.shape[0] // 2
    late_core, chip = lax.optimization_barrier((core, chip))
    weight_mine = crossed(lax.dynamic_slice_in_dim(out_weight, late_core * depth, depth, 0), ("xp",))

    q, cq, query_level = arranged(
        lax.axis_index("xp").reshape(1), (fine_query, fine_theirs, coarse_mine, coarse_theirs)
    )

    def folded(arrivals, state, last):
        blocks = [b for x in arrivals for b in (x, crossed(x, ("c",)))]
        return fold(q, cq, query_level, blocks, state, last, fine, coarse)

    state = fold(q, cq, query_level, [chip], None, False, fine, coarse)
    state, one, two = lax.optimization_barrier((state, one, two))
    three, four = along_z(one, 2), along_z(two[: two.shape[0] // 2], 2)
    state = folded((one, two), state, False)
    state, three, four = lax.optimization_barrier((state, three, four))
    state = folded((three, four), state, True)
    keep, to_xp, to_yl, to_both = state
    weight_mine, keep = lax.optimization_barrier((weight_mine, keep))
    weight_other = crossed(weight_mine, ("c",))
    near = crossed(to_yl, ("yl",))
    far = crossed(to_both, ("yl", "xp"))
    across = crossed(to_xp, ("xp",))
    rest = (HEAD[0], HEAD[2])
    n = lax.axis_size(rest)
    share = project(
        core.reshape(1),
        (keep, near, across, far),
        (out_weight, weight_mine, weight_other),
        fine // 2,
        n,
    )
    got = lax.all_to_all(share.reshape(n, -1, share.shape[1]), rest, 0, 0)
    return totals(got, got.shape[1] * fine // (fine + coarse))


def solution(mesh):
    torus = Mesh(
        mesh.devices.reshape(2, 8, 2, 2, 2, 2), ("yl", "z", "c", "yh", "xp", "xl")
    )
    placed = (
        P(CTX, HEAD),
        P(None, CTX, HEAD),
        P(CTX, HEAD),
        P(None, CTX, HEAD),
        P(CTX),
        P(HEAD, None),
    )
    return jax.shard_map(
        per_device,
        mesh=torus,
        in_specs=placed,
        out_specs=(P(CTX + HEAD, None), P(CTX + HEAD, None)),
        check_vma=False,
    )
```

profile of v0, /device:TPU:32, one launch (start us, length us, event | category | flops | bytes accessed | tf_op | source)
XLA Modules:
  0.0 109.2 jit_solution(16395114346441761833)
XLA Ops:
  0.6 0.7 convert_element_type.3
  1.3 1.0 fusion
  2.3 0.1 collective-permute-start
  2.4 1.4 %collective-permute-done = bf16[784,128]{1,0:T(8,128)(2,1)S(1)} collective-permute-done((bf16[784,128]{1,0:T(8,128)(2,1)S(1)}, bf16[784,128]{1,0:T(8,128)(2,1)S(1)}, u32[]{:S(2)}, u32[]{:S(2)}) %collective-permute-start) | collective-permute-done | bytes 200736 | tf_op jit(solution)/shard_map/ppermute | solution.py:220
  3.9 3.2 %constant_dynamic-slice_fusion = bf16[256,4096]{1,0:T(8,128)(2,1)} fusion(bf16[512,4096]{1,0:T(8,128)(2,1)} %w.1, s32[]{:T(128)S(6)} %select_n.3), kind=kLoop, calls=%fused_computation.3 | loop fusion | bytes 4194308 | tf_op jit(solution)/shard_map/dynamic_slice | solution.py:317
  7.1 3.0 %collective-permute-start.1 = (bf16[256,4096]{1,0:T(8,128)(2,1)}, bf16[256,4096]{1,0:T(8,128)(2,1)S(1)}, u32[]{:S(2)}, u32[]{:S(2)}) collective-permute-start(bf16[256,4096]{1,0:T(8,128)(2,1)} %constant_dynamic-slice_fusion), channel_id=1, source_target_pairs={{0,2},{2,0},{1,3},{3,1},{4,6},{6,4},{5,7},{7,5},{8,10},{10,8},{9,1... | collective-permute-start | bytes 6291464 | tf_op jit(solution)/shard_map/ppermute | solution.py:220
  10.1 1.9 %collective-permute-start.4 = (bf16[2,784,128]{2,1,0:T(8,128)(2,1)S(1)}, bf16[2,784,128]{2,1,0:T(8,128)(2,1)S(1)}, u32[]{:S(2)}, u32[]{:S(2)}) collective-permute-start(bf16[2,784,128]{2,1,0:T(8,128)(2,1)S(1)} %pad_maximum_fusion.refs_0_), channel_id=1, source_target_pairs={{0,16},{8,120},{16,32},{24,8},{32,48},{40,24},{48,64},{56,40},{64,... | collective-permute-start | bytes 1204232 | tf_op jit(solution)/shard_map/ppermute | solution.py:229
  12.0 4.5 %collective-permute-start.5 = (bf16[2,784,128]{2,1,0:T(8,128)(2,1)S(1)}, bf16[2,784,128]{2,1,0:T(8,128)(2,1)S(1)}, u32[]{:S(2)}, u32[]{:S(2)}) collective-permute-start(bf16[2,784,128]{2,1,0:T(8,128)(2,1)S(1)} %pad_maximum_fusion.refs_0_), channel_id=1, source_target_pairs={{0,32},{8,104},{16,48},{24,120},{32,64},{40,8},{48,80},{56,24},{64... | collective-permute-start | bytes 1204232 | tf_op jit(solution)/shard_map/ppermute | solution.py:229
  16.5 1.6 %collective-permute-start.2 = (bf16[256,512]{1,0:T(8,128)(2,1)}, bf16[256,512]{1,0:T(8,128)(2,1)}, u32[]{:S(2)}, u32[]{:S(2)}) collective-permute-start(bf16[256,512]{1,0:T(8,128)(2,1)} %fine_mine.1), channel_id=1, source_target_pairs={{0,128},{128,0},{1,129},{129,1},{2,130},{130,2},{3,131},{131,3},{4... | collective-permute-start | bytes 786440 | tf_op jit(solution)/shard_map/ppermute | solution.py:220
  18.1 0.1 broadcast_in_dim.5
  18.2 0.5 collective-permute-start.3
  18.7 9.1 %collective-permute-done.3.coarse_theirs = bf16[128,640]{1,0:T(8,128)(2,1)} collective-permute-done((bf16[128,640]{1,0:T(8,128)(2,1)S(1)}, bf16[128,640]{1,0:T(8,128)(2,1)}, u32[]{:S(2)}, u32[]{:S(2)}) %collective-permute-start.3) | collective-permute-done | bytes 163872 | tf_op jit(solution)/shard_map/ppermute | solution.py:220
  27.8 1.1 %arrange.1 = (bf16[512,512]{1,0:T(8,128)(2,1)S(1)}, bf16[256,512]{1,0:T(8,128)(2,1)S(1)}, f32[256,128]{1,0:T(8,128)S(1)}) custom-call(s32[1]{0:T(128)} %bitcast.5.xp_ref, bf16[256,512]{1,0:T(8,128)(2,1)} %fine_mine.1, bf16[256,512]{1,0:T(8,128)(2,1)} %collective-permute-done.2.fine_theirs, bf16[128,640]{1,0:T(8,128)(2,1)S(1)} %pad_maximum_fusion.2.coarse_mine, ...), custom_call_target="tpu_custom_call" | custom-call | bytes 1703936 | tf_op jit(solution)/shard_map/arrange/pallas_call | solution.py:259
  29.0 2.7 %fold.3 = (f32[4,512,128]{2,1,0:T(8,128)S(1)}, f32[4,512,256]{2,1,0:T(8,128)S(1)}, f32[4,256,128]{2,1,0:T(8,128)S(1)}, f32[4,256,256]{2,1,0:T(8,128)S(1)}) custom-call(bf16[512,512]{1,0:T(8,128)(2,1)S(1)} %get-tuple-element.34.q_ref, bf16[256,512]{1,0:T(8,128)(2,1)S(1)} %get-tuple-element.35.cq_ref, f32[256,128]{1,0:T(8,128)S(1)} %get-tuple-element.36.level_ref, ...), custom_call_target="tpu_custom_call" | custom-call | flops 1835008 | bytes 262144 | tf_op jit(solution)/shard_map/fold/pallas_call | solution.py:140
  31.7 0.1 collective-permute-start.6
  31.8 0.5 collective-permute-start.7
  32.3 3.5 %collective-permute-start.9 = (bf16[1,784,128]{2,1,0:T(8,128)(2,1)S(1)}, bf16[1,784,128]{2,1,0:T(8,128)(2,1)S(1)}, u32[]{:S(2)}, u32[]{:S(2)}) collective-permute-start(bf16[1,784,128]{2,1,0:T(8,128)(2,1)S(1)} %slice.3), channel_id=1, source_target_pairs={{0,32},{8,104},{16,48},{24,120},{32,64},{40,8},{48,80},{56,24},{64... | collective-permute-start | bytes 602120 | tf_op jit(solution)/shard_map/ppermute | solution.py:229
  35.9 10.1 %fold.4 = (f32[4,512,128]{2,1,0:T(8,128)S(1)}, f32[4,512,256]{2,1,0:T(8,128)S(1)}, f32[4,256,128]{2,1,0:T(8,128)S(1)}, f32[4,256,256]{2,1,0:T(8,128)S(1)}) custom-call(bf16[512,512]{1,0:T(8,128)(2,1)S(1)} %get-tuple-element.34.q_ref, ...), custom_call_target="tpu_custom_call", output_to_operand_aliasing={{0}: (7, {}), {1}: (8, {}), {2}: (9, {}), {3}: (10, {})} | custom-call | flops 7340032 | bytes 262144 | tf_op jit(solution)/shard_map/fold/pallas_call | solution.py:140
  45.9 4.5 %collective-permute-done.9.refs_2_ = bf16[1,784,128]{2,1,0:T(8,128)(2,1)S(1)} collective-permute-done((bf16[1,784,128]{2,1,0:T(8,128)(2,1)S(1)}, bf16[1,784,128]{2,1,0:T(8,128)(2,1)S(1)}, u32[]{:S(2)}, u32[]{:S(2)}) %collective-permute-start.9) | collective-permute-done | bytes 200736 | tf_op jit(solution)/shard_map/ppermute | solution.py:229
  50.5 0.5 collective-permute-start.11
  51.0 1.5 %collective-permute-done.11.refs_3_ = bf16[1,784,128]{2,1,0:T(8,128)(2,1)S(1)} collective-permute-done((bf16[1,784,128]{2,1,0:T(8,128)(2,1)S(1)}, bf16[1,784,128]{2,1,0:T(8,128)(2,1)S(1)}, u32[]{:S(2)}, u32[]{:S(2)}) %collective-permute-start.11) | collective-permute-done | bytes 200736 | tf_op jit(solution)/shard_map/ppermute | solution.py:220
  52.5 7.7 %fold.5 = (bf16[192,640]{1,0:T(8,128)(2,1)S(1)}, bf16[192,640]{1,0:T(8,128)(2,1)S(1)}, bf16[192,640]{1,0:T(8,128)(2,1)S(1)}, bf16[192,640]{1,0:T(8,128)(2,1)S(1)}) custom-call(bf16[512,512]{1,0:T(8,128)(2,1)S(1)} %get-tuple-element.34.q_ref, bf16[256,512]{1,0:T(8,128)(2,1)S(1)} %get-tuple-element.35.cq_ref, f32[256,128]{1,0:T(8,128)S(1)} %get-tuple-element.36.level_ref, ...), custom_call_target="tpu_custom_call" | custom-call | flops 5505024 | bytes 262144 | tf_op jit(solution)/shard_map/fold/pallas_call | solution.py:140
  60.2 0.2 collective-permute-start.15
  60.4 1.6 %collective-permute-start.12 = (bf16[192,640]{1,0:T(8,128)(2,1)S(1)}, bf16[192,640]{1,0:T(8,128)(2,1)S(1)}, u32[]{:S(2)}, u32[]{:S(2)}) collective-permute-start(bf16[192,640]{1,0:T(8,128)(2,1)S(1)} %get-tuple-element.60), channel_id=1, source_target_pairs={{0,128},{128,0},{1,129},{129,1},{2,130},{130,2},{3,131},{131,3},{4... | collective-permute-start | bytes 737288 | tf_op jit(solution)/shard_map/ppermute | solution.py:220
  62.0 0.5 collective-permute-start.13
  62.5 2.9 %collective-permute-start.14 = (bf16[192,640]{1,0:T(8,128)(2,1)S(1)}, bf16[192,640]{1,0:T(8,128)(2,1)S(1)}, u32[]{:S(2)}, u32[]{:S(2)}) collective-permute-start(bf16[192,640]{1,0:T(8,128)(2,1)S(1)} %get-tuple-element.62), channel_id=1, source_target_pairs={{0,130},{2,128},{128,2},{130,0},{1,131},{3,129},{129,3},{131,1},{4... | collective-permute-start | bytes 737288 | tf_op jit(solution)/shard_map/ppermute | solution.py:220
  65.4 3.2 %collective-permute-done.12.near = bf16[192,640]{1,0:T(8,128)(2,1)S(1)} collective-permute-done((bf16[192,640]{1,0:T(8,128)(2,1)S(1)}, bf16[192,640]{1,0:T(8,128)(2,1)S(1)}, u32[]{:S(2)}, u32[]{:S(2)}) %collective-permute-start.12) | collective-permute-done | bytes 245792 | tf_op jit(solution)/shard_map/ppermute | solution.py:220
  68.6 3.7 %collective-permute-done.13.cross = bf16[192,640]{1,0:T(8,128)(2,1)S(1)} collective-permute-done((bf16[192,640]{1,0:T(8,128)(2,1)S(1)}, bf16[192,640]{1,0:T(8,128)(2,1)S(1)}, u32[]{:S(2)}, u32[]{:S(2)}) %collective-permute-start.13) | collective-permute-done | bytes 245792 | tf_op jit(solution)/shard_map/ppermute | solution.py:220
  72.3 4.3 %collective-permute-done.14.far = bf16[192,640]{1,0:T(8,128)(2,1)S(1)} collective-permute-done((bf16[192,640]{1,0:T(8,128)(2,1)S(1)}, bf16[192,640]{1,0:T(8,128)(2,1)S(1)}, u32[]{:S(2)}, u32[]{:S(2)}) %collective-permute-start.14) | collective-permute-done | bytes 245792 | tf_op jit(solution)/shard_map/ppermute | solution.py:220
  76.6 4.2 %project.1 = bf16[192,4096]{1,0:T(8,128)(2,1)S(1)} custom-call(s32[1]{0:T(128)} %bitcast.core_ref, bf16[192,640]{1,0:T(8,128)(2,1)S(1)} %get-tuple-element.59.keep, bf16[192,640]{1,0:T(8,128)(2,1)S(1)} %collective-permute-done.12.near, bf16[192,640]{1,0:T(8,128)(2,1)S(1)} %collective-permute-done.13.cross, bf16[192,640]{1,0:T(8,128)(2,1)S(1)} %collective-permute-done.14.far, ...), custom_call_target="tpu_custom_call" | custom-call | flops 1610612736 | bytes 8388608 | tf_op jit(solution)/shard_map/project/pallas_call | solution.py:201
  80.8 25.0 %all_to_all.5.got = bf16[4,48,4096]{2,1,0:T(8,128)(2,1)} all-to-all(bf16[4,48,4096]{2,1,0:T(8,128)(2,1)S(1)} %bitcast.8), channel_id=1, replica_groups=mesh['yl'=2,'z'=8,'c'=2,'yh'=2,'xp'=2,'xl'=2] {'yh','xl'}, dimensions={0} | all-to-all | bytes 3145728 | tf_op jit(solution)/shard_map/all_to_all | solution.py:348
  105.8 3.4 %totals.1 = (bf16[32,4096]{1,0:T(8,128)(2,1)}, bf16[16,4096]{1,0:T(8,128)(2,1)}) custom-call(bf16[4,48,4096]{2,1,0:T(8,128)(2,1)} %all_to_all.5.got), custom_call_target="tpu_custom_call" | custom-call | flops 786432 | bytes 2359296 | tf_op jit(solution)/shard_map/totals/pallas_call | solution.py:284
  (19 shorter events, 0.1 us)
Async XLA Ops:
  2.3 1.5 %collective-permute-start = (bf16[784,128]{1,0:T(8,128)(2,1)S(1)}, bf16[784,128]{1,0:T(8,128)(2,1)S(1)}, u32[]{:S(2)}, u32[]{:S(2)}) collective-permute-start(bf16[784,128]{1,0:T(8,128)(2,1)S(1)} %get-tuple-element.65), channel_id=1, source_target_pairs={{0,8},{8,0},{1,9},{9,1},{2,10},{10,2},{3,11},{11,3},{4,12},{12,4},... | collective-permute-start | bytes 602120 | tf_op jit(solution)/shard_map/ppermute | solution.py:220
  3.9 14.3 %copy-start.1 = (bf16[128,512]{1,0:T(8,128)(2,1)S(1)}, bf16[128,512]{1,0:T(8,128)(2,1)}, u32[]{:S(2)}) copy-start(bf16[128,512]{1,0:T(8,128)(2,1)} %param.8) | copy-start | bytes 393220
  7.1 53.1 %collective-permute-start.1 = (bf16[256,4096]{1,0:T(8,128)(2,1)}, bf16[256,4096]{1,0:T(8,128)(2,1)S(1)}, u32[]{:S(2)}, u32[]{:S(2)}) collective-permute-start(bf16[256,4096]{1,0:T(8,128)(2,1)} %constant_dynamic-slice_fusion), channel_id=1, source_target_pairs={{0,2},{2,0},{1,3},{3,1},{4,6},{6,4},{5,7},{7,5},{8,10},{10,8},{9,1... | collective-permute-start | bytes 6291464 | tf_op jit(solution)/shard_map/ppermute | solution.py:220
  10.1 21.6 %collective-permute-start.4 = (bf16[2,784,128]{2,1,0:T(8,128)(2,1)S(1)}, bf16[2,784,128]{2,1,0:T(8,128)(2,1)S(1)}, u32[]{:S(2)}, u32[]{:S(2)}) collective-permute-start(bf16[2,784,128]{2,1,0:T(8,128)(2,1)S(1)} %pad_maximum_fusion.refs_0_), channel_id=1, source_target_pairs={{0,16},{8,120},{16,32},{24,8},{32,48},{40,24},{48,64},{56,40},{64,... | collective-permute-start | bytes 1204232 | tf_op jit(solution)/shard_map/ppermute | solution.py:229
  12.0 19.7 %collective-permute-start.5 = (bf16[2,784,128]{2,1,0:T(8,128)(2,1)S(1)}, bf16[2,784,128]{2,1,0:T(8,128)(2,1)S(1)}, u32[]{:S(2)}, u32[]{:S(2)}) collective-permute-start(bf16[2,784,128]{2,1,0:T(8,128)(2,1)S(1)} %pad_maximum_fusion.refs_0_), channel_id=1, source_target_pairs={{0,32},{8,104},{16,48},{24,120},{32,64},{40,8},{48,80},{56,24},{64... | collective-permute-start | bytes 1204232 | tf_op jit(solution)/shard_map/ppermute | solution.py:229
  16.5 11.3 %collective-permute-start.2 = (bf16[256,512]{1,0:T(8,128)(2,1)}, bf16[256,512]{1,0:T(8,128)(2,1)}, u32[]{:S(2)}, u32[]{:S(2)}) collective-permute-start(bf16[256,512]{1,0:T(8,128)(2,1)} %fine_mine.1), channel_id=1, source_target_pairs={{0,128},{128,0},{1,129},{129,1},{2,130},{130,2},{3,131},{131,3},{4... | collective-permute-start | bytes 786440 | tf_op jit(solution)/shard_map/ppermute | solution.py:220
  18.2 9.6 %collective-permute-start.3 = (bf16[128,640]{1,0:T(8,128)(2,1)S(1)}, bf16[128,640]{1,0:T(8,128)(2,1)}, u32[]{:S(2)}, u32[]{:S(2)}) collective-permute-start(bf16[128,640]{1,0:T(8,128)(2,1)S(1)} %pad_maximum_fusion.2.coarse_mine), channel_id=1, source_target_pairs={{0,128},{128,0},{1,129},{129,1},{2,130},{130,2},{3,131},{131,3},{4... | collective-permute-start | bytes 491528 | tf_op jit(solution)/shard_map/ppermute | solution.py:220
  31.7 4.1 %collective-permute-start.6 = (bf16[2,784,128]{2,1,0:T(8,128)(2,1)S(1)}, bf16[2,784,128]{2,1,0:T(8,128)(2,1)S(1)}, u32[]{:S(2)}, u32[]{:S(2)}) collective-permute-start(bf16[2,784,128]{2,1,0:T(8,128)(2,1)S(1)} %collective-permute-done.4.refs_0_), channel_id=1, source_target_pairs={{0,8},{8,0},{1,9},{9,1},{2,10},{10,2},{3,11},{11,3},{4,12},{12,4},... | collective-permute-start | bytes 1204232 | tf_op jit(solution)/shard_map/ppermute | solution.py:220
  31.8 4.0 %collective-permute-start.7 = (bf16[2,784,128]{2,1,0:T(8,128)(2,1)S(1)}, bf16[2,784,128]{2,1,0:T(8,128)(2,1)S(1)}, u32[]{:S(2)}, u32[]{:S(2)}) collective-permute-start(bf16[2,784,128]{2,1,0:T(8,128)(2,1)S(1)} %collective-permute-done.5.refs_2_), channel_id=1, source_target_pairs={{0,8},{8,0},{1,9},{9,1},{2,10},{10,2},{3,11},{11,3},{4,12},{12,4},... | collective-permute-start | bytes 1204232 | tf_op jit(solution)/shard_map/ppermute | solution.py:220
  32.3 18.1 %collective-permute-start.8 = (bf16[2,784,128]{2,1,0:T(8,128)(2,1)S(1)}, bf16[2,784,128]{2,1,0:T(8,128)(2,1)S(1)}, u32[]{:S(2)}, u32[]{:S(2)}) collective-permute-start(bf16[2,784,128]{2,1,0:T(8,128)(2,1)S(1)} %collective-permute-done.4.refs_0_), channel_id=1, source_target_pairs={{0,32},{8,104},{16,48},{24,120},{32,64},{40,8},{48,80},{56,24},{64... | collective-permute-start | bytes 1204232 | tf_op jit(solution)/shard_map/ppermute | solution.py:229
  32.3 18.1 %collective-permute-start.9 = (bf16[1,784,128]{2,1,0:T(8,128)(2,1)S(1)}, bf16[1,784,128]{2,1,0:T(8,128)(2,1)S(1)}, u32[]{:S(2)}, u32[]{:S(2)}) collective-permute-start(bf16[1,784,128]{2,1,0:T(8,128)(2,1)S(1)} %slice.3), channel_id=1, source_target_pairs={{0,32},{8,104},{16,48},{24,120},{32,64},{40,8},{48,80},{56,24},{64... | collective-permute-start | bytes 602120 | tf_op jit(solution)/shard_map/ppermute | solution.py:229
  50.5 26.1 %copy-start = (bf16[512,4096]{1,0:T(8,128)(2,1)S(1)}, bf16[512,4096]{1,0:T(8,128)(2,1)}, u32[]{:S(2)}) copy-start(bf16[512,4096]{1,0:T(8,128)(2,1)} %w.1) | copy-start | bytes 12582916
  50.5 2.0 %collective-permute-start.10 = (bf16[2,784,128]{2,1,0:T(8,128)(2,1)S(1)}, bf16[2,784,128]{2,1,0:T(8,128)(2,1)S(1)}, u32[]{:S(2)}, u32[]{:S(2)}) collective-permute-start(bf16[2,784,128]{2,1,0:T(8,128)(2,1)S(1)} %collective-permute-done.8.refs_0_), channel_id=1, source_target_pairs={{0,8},{8,0},{1,9},{9,1},{2,10},{10,2},{3,11},{11,3},{4,12},{12,4},... | collective-permute-start | bytes 1204232 | tf_op jit(solution)/shard_map/ppermute | solution.py:220
  50.5 2.0 %collective-permute-start.11 = (bf16[1,784,128]{2,1,0:T(8,128)(2,1)S(1)}, bf16[1,784,128]{2,1,0:T(8,128)(2,1)S(1)}, u32[]{:S(2)}, u32[]{:S(2)}) collective-permute-start(bf16[1,784,128]{2,1,0:T(8,128)(2,1)S(1)} %collective-permute-done.9.refs_2_), channel_id=1, source_target_pairs={{0,8},{8,0},{1,9},{9,1},{2,10},{10,2},{3,11},{11,3},{4,12},{12,4},... | collective-permute-start | bytes 602120 | tf_op jit(solution)/shard_map/ppermute | solution.py:220
  60.2 16.4 %collective-permute-start.15 = (bf16[256,4096]{1,0:T(8,128)(2,1)S(1)}, bf16[256,4096]{1,0:T(8,128)(2,1)S(1)}, u32[]{:S(2)}, u32[]{:S(2)}) collective-permute-start(bf16[256,4096]{1,0:T(8,128)(2,1)S(1)} %collective-permute-done.1.w_mine), channel_id=1, source_target_pairs={{0,8},{8,0},{1,9},{9,1},{2,10},{10,2},{3,11},{11,3},{4,12},{12,4},... | collective-permute-start | bytes 6291464 | tf_op jit(solution)/shard_map/ppermute | solution.py:220
  60.4 8.2 %collective-permute-start.12 = (bf16[192,640]{1,0:T(8,128)(2,1)S(1)}, bf16[192,640]{1,0:T(8,128)(2,1)S(1)}, u32[]{:S(2)}, u32[]{:S(2)}) collective-permute-start(bf16[192,640]{1,0:T(8,128)(2,1)S(1)} %get-tuple-element.60), channel_id=1, source_target_pairs={{0,128},{128,0},{1,129},{129,1},{2,130},{130,2},{3,131},{131,3},{4... | collective-permute-start | bytes 737288 | tf_op jit(solution)/shard_map/ppermute | solution.py:220
  62.0 10.3 %collective-permute-start.13 = (bf16[192,640]{1,0:T(8,128)(2,1)S(1)}, bf16[192,640]{1,0:T(8,128)(2,1)S(1)}, u32[]{:S(2)}, u32[]{:S(2)}) collective-permute-start(bf16[192,640]{1,0:T(8,128)(2,1)S(1)} %get-tuple-element.61), channel_id=1, source_target_pairs={{0,2},{2,0},{1,3},{3,1},{4,6},{6,4},{5,7},{7,5},{8,10},{10,8},{9,1... | collective-permute-start | bytes 737288 | tf_op jit(solution)/shard_map/ppermute | solution.py:220
  62.5 14.1 %collective-permute-start.14 = (bf16[192,640]{1,0:T(8,128)(2,1)S(1)}, bf16[192,640]{1,0:T(8,128)(2,1)S(1)}, u32[]{:S(2)}, u32[]{:S(2)}) collective-permute-start(bf16[192,640]{1,0:T(8,128)(2,1)S(1)} %get-tuple-element.62), channel_id=1, source_target_pairs={{0,130},{2,128},{128,2},{130,0},{1,131},{3,129},{129,3},{131,1},{4... | collective-permute-start | bytes 737288 | tf_op jit(solution)/shard_map/ppermute | solution.py:220
where the time goes:
time: 109 us
  Pallas kernels  29.1 us (27%)
  waiting for transfers between devices  27.8 us (26%)
  blocking collectives  25 us (23%)
  starting transfers between devices  21.5 us (20%)
  local copies, waits for them, and re-layouts  3.29 us (3%)
  other arithmetic  1.71 us (2%)
    all_to_all x1, blocking collectives, per_device(): got = lax.all_to_all(share.reshape(n, -1, share.shape[1]), rest, 0, 0)  25 us
    ppermute x12, waiting for transfers between devices, crossed(): return lax.ppermute(x, axes, [(i, n - 1 - i) for i in range(n)])  23.2 us
    pallas_call x3, Pallas kernels, fold(): pl.pallas_call(functools.partial(fold_kernel, len(blocks), fine, coarse,...  20.4 us
    ppermute x12, starting transfers between devices, crossed(): return lax.ppermute(x, axes, [(i, n - 1 - i) for i in range(n)])  11.6 us
    ppermute x4, starting transfers between devices, along_z(): return lax.ppermute(x, ('z', 'c'), pairs)  9.91 us
    ppermute x4, waiting for transfers between devices, along_z(): return lax.ppermute(x, ('z', 'c'), pairs)  4.55 us
    pallas_call x1, Pallas kernels, project(): pl.pallas_call(functools.partial(project_kernel, n_fine, n_blocks), grid=...  4.19 us
    pallas_call x1, Pallas kernels, totals(): pl.pallas_call(functools.partial(total_kernel), grid=(columns // tile,),...  3.36 us
  transfers between devices with their start and end apart: 16, of which 7 were waited for; matrix products, arithmetic and copies ran while one was open for 0% of the time, Pallas kernels for 20%

commit v1 on v0

--- a/solution.py
+++ b/solution.py
@@ -46,7 +46,8 @@
     return result.astype(jnp.bfloat16)
 
 
-def fold_kernel(n_blocks, fine, coarse, first, last, tile, q_ref, cq_ref, level_ref, *refs):
+def fold_kernel(n_blocks, fine, coarse, first, part, q_ref, cq_ref, level_ref, *refs):
+    last = part is not None
     blocks, refs = refs[:n_blocks], refs[n_blocks:]
     if not first:
         state, refs = refs[:4], refs[4:]
@@ -66,6 +67,7 @@
     n_fine = k.shape[0] - key_level.shape[1]
 
     def attend(queries, keys, values, allowed, h, rows, m_in, acc_in, m_out, acc_out):
+        tile = rows.stop - rows.start
         s = dot_nt(queries[rows, h * HD : (h + 1) * HD], keys)
         if allowed is not None:
             s = jnp.where(allowed, s, LOW)
@@ -85,14 +87,17 @@
             return None
         return (acc[:, :HD] / acc[:, HD:]).astype(jnp.bfloat16), new, acc[:, HD:]
 
-    lane = lax.broadcasted_iota(jnp.int32, (tile, HD), 1)
     for is_coarse in (False, True):
         queries = cq_ref if is_coarse else q_ref
         pair = 2 if is_coarse else 0
         m_in, acc_in = (None, None) if first else state[pair : pair + 2]
         m_out, acc_out = (None, None) if last else refs[pair : pair + 2]
-        for t in range(queries.shape[0] // tile):
-            rows = slice(t * tile, (t + 1) * tile)
+        half = queries.shape[0] // 2
+        tile = min(TILE, half)
+        lane = lax.broadcasted_iota(jnp.int32, (tile, HD), 1)
+        begin, end = (part * half, (part + 1) * half) if last else (0, 2 * half)
+        for start in range(begin, end, tile):
+            rows = slice(start, start + tile)
             if is_coarse:
                 allowed = key_level <= level_ref[rows, :1]
                 keys, values = k[n_fine:], v[n_fine:]
@@ -103,32 +108,33 @@
             for h in range(heads):
                 done = attend(queries, keys, values, allowed, h, rows, m_in, acc_in, m_out, acc_out)
                 if last:
-                    place(refs, is_coarse, t, tile, q_ref.shape[0] // 4, h, done[0])
+                    place(refs, is_coarse, start - begin, q_ref.shape[0] // 4, h, done[0])
                     top = jnp.where(lane // 3 == h, done[1], top)
                     total = jnp.where(lane // 3 == h, done[2], total)
             if last:
                 stats = in_three(top * EXPONENT + jnp.log(total) * math.log2(math.e), lane % 3)
-                place(refs, is_coarse, t, tile, q_ref.shape[0] // 4, heads, stats)
-
-
-def place(outs, is_coarse, t, tile, n_fine, h, value):
+                place(refs, is_coarse, start - begin, q_ref.shape[0] // 4, heads, stats)
+
+
+def place(outs, is_coarse, begin, n_fine, h, value):
     n = outs[0].shape[0] - n_fine if is_coarse else n_fine
-    for i in range(max(1, tile // n)):
-        row = t * tile + i * n
+    length = min(n, value.shape[0])
+    for i in range(value.shape[0] // length):
+        row = begin + i * length
         start = row % n + (n_fine if is_coarse else 0)
-        length = min(n, tile)
         outs[row // n][start : start + length, h * HD : (h + 1) * HD] = value[
-            i * n : i * n + length
+            i * length : (i + 1) * length
         ]
 
 
-def fold(q, cq, level, blocks, state, last, fine, coarse):
+def fold(q, cq, level, blocks, state, part, fine, coarse):
     heads = q.shape[1] // HD
     first = state is None
     ins = (q, cq, level, *blocks, *(() if first else state))
+    last = part is not None
     if last:
         quarter = (q.shape[0] + cq.shape[0]) // 4
-        out = (jax.ShapeDtypeStruct((quarter, q.shape[1] + HD), jnp.bfloat16),) * 4
+        out = (jax.ShapeDtypeStruct((quarter, q.shape[1] + HD), jnp.bfloat16),) * 2
     else:
         out = tuple(
             jax.ShapeDtypeStruct((heads, rows, width), jnp.float32)
@@ -138,20 +144,21 @@
     work = heads * sum(b.shape[0] for b in blocks) * (q.shape[0] * (fine + coarse) + cq.shape[0] * coarse)
     aliases = {} if first or last else {len(ins) - 4 + i: i for i in range(4)}
     return pl.pallas_call(
-        functools.partial(fold_kernel, len(blocks), fine, coarse, first, last, TILE),
+        functools.partial(fold_kernel, len(blocks), fine, coarse, first, part),
         out_shape=out,
         in_specs=[whole(a.shape) for a in ins],
         out_specs=tuple(whole(o.shape) for o in out),
         input_output_aliases=aliases,
         compiler_params=pltpu.CompilerParams(vmem_limit_bytes=GRANT),
         cost_estimate=pl.CostEstimate(
-            flops=work, bytes_accessed=q.size, transcendentals=0
+            flops=8 * work * HD, bytes_accessed=q.size, transcendentals=0
         ),
         name="fold",
     )(*ins)
 
 
-def project_kernel(n_fine, n_blocks, core_ref, keep, near, cross, far, w, w_mine, w_other, o_ref, a_ref):
+def project_kernel(n_fine, n_blocks, place_ref, keep, near, cross, far, w, w_mine, w_other, *refs):
+    outs, a_ref = refs[:-1], refs[-1]
     heads = keep.shape[1] // HD - 1
     rows = keep.shape[0]
     width = heads * HD
@@ -159,7 +166,7 @@
 
     @pl.when(pl.program_id(0) == 0)
     def _():
-        swap = jnp.broadcast_to(core_ref[0], (1, 1)) == 1
+        swap = jnp.broadcast_to(place_ref[0], (1, 1)) == 1
         for g, (one, two) in enumerate(((keep, near), (cross, far))):
             merged = []
             for h in range(heads):
@@ -181,19 +188,24 @@
             n_coarse = rows - n_fine
             f, c = n_fine // n_blocks, n_coarse // n_blocks
             for b in range(n_blocks):
-                at = b * (f + c)
+                at = jnp.bitwise_xor(place_ref[1], b) * (f + c)
                 cols = slice(g * width, (g + 1) * width)
-                a_ref[at : at + f, cols] = merged[b * f : (b + 1) * f]
-                a_ref[at + f : at + f + c, cols] = merged[n_fine + b * c : n_fine + (b + 1) * c]
-
-    o_ref[...] = (
+                a_ref[pl.ds(pl.multiple_of(at, c), f), cols] = merged[b * f : (b + 1) * f]
+                a_ref[pl.ds(pl.multiple_of(at + f, c), c), cols] = merged[
+                    n_fine + b * c : n_fine + (b + 1) * c
+                ]
+
+    share = (
         dot_nn(a_ref[:, :width], w[...])
         + dot_nn(a_ref[:, width : width + half], w_mine[...])
         + dot_nn(a_ref[:, width + half :], w_other[...])
     ).astype(jnp.bfloat16)
-
-
-def project(core, parts, weights, n_fine, n_blocks):
+    size = rows // n_blocks
+    for i, out in enumerate(outs):
+        out[...] = share[i * size : (i + 1) * size]
+
+
+def project(places, parts, weights, n_fine, n_blocks):
     rows = parts[0].shape[0]
     columns = weights[0].shape[1]
     tile = math.gcd(columns, 1024)
@@ -201,18 +213,18 @@
     return pl.pallas_call(
         functools.partial(project_kernel, n_fine, n_blocks),
         grid=(columns // tile,),
-        out_shape=jax.ShapeDtypeStruct((rows, columns), jnp.bfloat16),
+        out_shape=(jax.ShapeDtypeStruct((rows // n_blocks, columns), jnp.bfloat16),) * n_blocks,
         in_specs=[pl.BlockSpec(memory_space=pltpu.SMEM)]
         + [whole(p.shape) for p in parts]
         + [pl.BlockSpec((w.shape[0], tile), lambda j: (0, j)) for w in weights],
-        out_specs=pl.BlockSpec((rows, tile), lambda j: (0, j)),
+        out_specs=(pl.BlockSpec((rows // n_blocks, tile), lambda j: (0, j)),) * n_blocks,
         scratch_shapes=[pltpu.VMEM((rows, depth), jnp.bfloat16)],
         compiler_params=pltpu.CompilerParams(vmem_limit_bytes=GRANT),
         cost_estimate=pl.CostEstimate(
             flops=2 * rows * depth * columns, bytes_accessed=2 * depth * columns, transcendentals=0
         ),
         name="project",
-    )(core, *parts, *weights)
+    )(places, *parts, *weights)
 
 
 def crossed(x, axes):
@@ -269,31 +281,6 @@
     )(xp, *arrays)
 
 
-def total_kernel(got, first, second):
-    n = first.shape[0]
-    total = got[0].astype(jnp.float32)
-    for i in range(1, got.shape[0]):
-        total = total + got[i].astype(jnp.float32)
-    first[...] = total[:n].astype(jnp.bfloat16)
-    second[...] = total[n:].astype(jnp.bfloat16)
-
-
-def totals(got, n):
-    parts, rows, columns = got.shape
-    tile = math.gcd(columns, 1024)
-    return pl.pallas_call(
-        functools.partial(total_kernel),
-        grid=(columns // tile,),
-        out_shape=tuple(
-            jax.ShapeDtypeStruct((r, columns), jnp.bfloat16) for r in (n, rows - n)
-        ),
-        in_specs=[pl.BlockSpec((parts, rows, tile), lambda j: (0, 0, j))],
-        out_specs=tuple(pl.BlockSpec((r, tile), lambda j: (0, j)) for r in (n, rows - n)),
-        cost_estimate=pl.CostEstimate(flops=got.size, bytes_accessed=3 * got.size, transcendentals=0),
-        name="totals",
-    )(got)
-
-
 def per_device(fine_query, fine_memory, coarse_query, coarse_memory, coarse_scale, out_weight):
     fine, coarse = fine_query.shape[0], coarse_query.shape[0]
     width = fine_query.shape[1]
@@ -313,40 +300,46 @@
 
     core = lax.axis_index("c")
     depth = out_weight.shape[0] // 2
-    late_core, chip = lax.optimization_barrier((core, chip))
-    weight_mine = crossed(lax.dynamic_slice_in_dim(out_weight, late_core * depth, depth, 0), ("xp",))
+    weight_mine = crossed(lax.dynamic_slice_in_dim(out_weight, core * depth, depth, 0), ("xp",))
 
     q, cq, query_level = arranged(
         lax.axis_index("xp").reshape(1), (fine_query, fine_theirs, coarse_mine, coarse_theirs)
     )
 
-    def folded(arrivals, state, last):
-        blocks = [b for x in arrivals for b in (x, crossed(x, ("c",)))]
-        return fold(q, cq, query_level, blocks, state, last, fine, coarse)
-
-    state = fold(q, cq, query_level, [chip], None, False, fine, coarse)
+    def folded(blocks, state, part):
+        return fold(q, cq, query_level, blocks, state, part, fine, coarse)
+
+    def with_twins(arrivals):
+        return [b for x in arrivals for b in (x, crossed(x, ("c",)))]
+
+    state = folded([chip], None, None)
     state, one, two = lax.optimization_barrier((state, one, two))
     three, four = along_z(one, 2), along_z(two[: two.shape[0] // 2], 2)
-    state = folded((one, two), state, False)
+    state = folded(with_twins((one, two)), state, None)
     state, three, four = lax.optimization_barrier((state, three, four))
-    state = folded((three, four), state, True)
-    keep, to_xp, to_yl, to_both = state
+    blocks = with_twins((three, four))
+    to_yl, to_both = folded(blocks, state, 1)
+    near, far = crossed(to_yl, ("yl",)), crossed(to_both, ("yl", "xp"))
+    keep, to_xp = folded(blocks, state, 0)
+    across = crossed(to_xp, ("xp",))
     weight_mine, keep = lax.optimization_barrier((weight_mine, keep))
     weight_other = crossed(weight_mine, ("c",))
-    near = crossed(to_yl, ("yl",))
-    far = crossed(to_both, ("yl", "xp"))
-    across = crossed(to_xp, ("xp",))
-    rest = (HEAD[0], HEAD[2])
-    n = lax.axis_size(rest)
-    share = project(
-        core.reshape(1),
+    shares = project(
+        jnp.stack([core, lax.axis_index((HEAD[0], HEAD[2]))]),
         (keep, near, across, far),
         (out_weight, weight_mine, weight_other),
         fine // 2,
-        n,
-    )
-    got = lax.all_to_all(share.reshape(n, -1, share.shape[1]), rest, 0, 0)
-    return totals(got, got.shape[1] * fine // (fine + coarse))
+        4,
+    )
+    got = [shares[0]]
+    for share, axes in zip(shares[1:], ((HEAD[2],), (HEAD[0],), (HEAD[0], HEAD[2]))):
+        got.append(crossed(share, axes))
+    split = got[0].shape[0] * fine // (fine + coarse)
+
+    def total(rows):
+        return sum(g[rows].astype(jnp.float32) for g in got).astype(jnp.bfloat16)
+
+    return total(slice(0, split)), total(slice(split, None))
 
 
 def solution(mesh):

time: 109 us -> 117 us (1.073)
  blocking collectives: 25 us -> 0 us
  waiting for transfers between devices: 27.8 us -> 47 us
  starting transfers between devices: 21.5 us -> 28.3 us
  local copies, waits for them, and re-layouts: 3.29 us -> 6.36 us
  other arithmetic: 1.71 us -> 4.25 us
    all_to_all x1 -> x0, blocking collectives: 25 us -> none  [per_device(): got = lax.all_to_all(share.reshape(n, -1, share.shape[1]), rest, 0, 0)]
    ppermute x12 -> x15, waiting for transfers between devices: 23.2 us -> 42.6 us  [crossed(): return lax.ppermute(x, axes, [(i, n - 1 - i) for i in range(n)])]
    ppermute x12 -> x15, starting transfers between devices: 11.6 us -> 16.4 us  [crossed(): return lax.ppermute(x, axes, [(i, n - 1 - i) for i in range(n)])]
    pallas_call x3 -> x4, Pallas kernels: 20.4 us -> 24.4 us  [fold(): pl.pallas_call(functools.partial(fold_kernel, len(blocks), fine, coarse,...]
    pallas_call x1 -> x0, Pallas kernels: 3.36 us -> none  [totals(): pl.pallas_call(functools.partial(total_kernel), grid=(columns // tile,),...]
    unnamed x4, local copies, waits for them, and re-layouts: 0.01 us -> 2.2 us
    ppermute x4, starting transfers between devices: 9.91 us -> 11.9 us  [along_z(): return lax.ppermute(x, ('z', 'c'), pairs)]
    convert_element_type x0 -> x2, other arithmetic: none -> 1.56 us  [total(): return sum((g[rows].astype(jnp.float32) for g in got)).astype(jnp.bfloat16)]
  transfers between devices with their start and end apart: 16 -> 19, of which waited for: 7 -> 8; matrix products, arithmetic and copies ran while one was open for 0% -> 4% of each run, Pallas kernels for 20% -> 21%
where the time goes in v1:
time: 117 us
  waiting for transfers between devices  47 us (40%)
  Pallas kernels  30 us (26%)
  starting transfers between devices  28.3 us (24%)
  local copies, waits for them, and re-layouts  6.36 us (5%)
  other arithmetic  4.25 us (4%)
    ppermute x15, waiting for transfers between devices, crossed(): return lax.ppermute(x, axes, [(i, n - 1 - i) for i in range(n)])  42.6 us
    pallas_call x4, Pallas kernels, fold(): pl.pallas_call(functools.partial(fold_kernel, len(blocks), fine, coarse,...  24.4 us
    ppermute x15, starting transfers between devices, crossed(): return lax.ppermute(x, axes, [(i, n - 1 - i) for i in range(n)])  16.4 us
    ppermute x4, starting transfers between devices, along_z(): return lax.ppermute(x, ('z', 'c'), pairs)  11.9 us
    pallas_call x1, Pallas kernels, project(): pl.pallas_call(functools.partial(project_kernel, n_fine, n_blocks), grid=...  5.53 us
    ppermute x4, waiting for transfers between devices, along_z(): return lax.ppermute(x, ('z', 'c'), pairs)  4.34 us
    dynamic_slice x1, local copies, waits for them, and re-layouts, per_device(): lax.dynamic_slice_in_dim(out_weight, core * depth, depth, 0)  3.14 us
  transfers between devices with their start and end apart: 19, of which 8 were waited for; matrix products, arithmetic and copies ran while one was open for 4% of the time, Pallas kernels for 21%

profile of v1, /device:TPU:32, one launch (start us, length us, event | category | flops | bytes accessed | tf_op | source)
XLA Modules:
  0.0 116.5 jit_solution(17194283314881689813)
XLA Ops:
  0.6 0.7 convert_element_type.33
  1.3 1.0 fusion
  2.5 0.9 pad_maximum_fusion.2.coarse_mine
  3.4 1.7 %collective-permute-start.2 = (bf16[128,640]{1,0:T(8,128)(2,1)S(1)}, bf16[128,640]{1,0:T(8,128)(2,1)S(1)}, u32[]{:S(2)}, u32[]{:S(2)}) collective-permute-start(bf16[128,640]{1,0:T(8,128)(2,1)S(1)} %pad_maximum_fusion.2.coarse_mine), channel_id=1, source_target_pairs={{0,128},{128,0},{1,129},{129,1},{2,130},{130,2},{3,131},{131,3},{4... | collective-permute-start | bytes 491528 | tf_op jit(solution)/shard_map/ppermute | solution.py:232
  5.6 2.0 %collective-permute-start.4 = (bf16[2,784,128]{2,1,0:T(8,128)(2,1)S(1)}, bf16[2,784,128]{2,1,0:T(8,128)(2,1)}, u32[]{:S(2)}, u32[]{:S(2)}) collective-permute-start(bf16[2,784,128]{2,1,0:T(8,128)(2,1)S(1)} %pad_maximum_fusion.refs_0_), channel_id=1, source_target_pairs={{0,16},{8,120},{16,32},{24,8},{32,48},{40,24},{48,64},{56,40},{64,... | collective-permute-start | bytes 1204232 | tf_op jit(solution)/shard_map/ppermute | solution.py:241
  7.6 4.5 %collective-permute-start.5 = (bf16[2,784,128]{2,1,0:T(8,128)(2,1)S(1)}, bf16[2,784,128]{2,1,0:T(8,128)(2,1)}, u32[]{:S(2)}, u32[]{:S(2)}) collective-permute-start(bf16[2,784,128]{2,1,0:T(8,128)(2,1)S(1)} %pad_maximum_fusion.refs_0_), channel_id=1, source_target_pairs={{0,32},{8,104},{16,48},{24,120},{32,64},{40,8},{48,80},{56,24},{64... | collective-permute-start | bytes 1204232 | tf_op jit(solution)/shard_map/ppermute | solution.py:241
  12.1 3.1 %constant_dynamic-slice_fusion = bf16[256,4096]{1,0:T(8,128)(2,1)} fusion(bf16[512,4096]{1,0:T(8,128)(2,1)} %w.1, s32[]{:T(128)S(6)} %select_n.3), kind=kLoop, calls=%fused_computation.6 | loop fusion | bytes 4194308 | tf_op jit(solution)/shard_map/dynamic_slice | solution.py:303
  15.2 3.0 %collective-permute-start = (bf16[256,4096]{1,0:T(8,128)(2,1)}, bf16[256,4096]{1,0:T(8,128)(2,1)S(1)}, u32[]{:S(2)}, u32[]{:S(2)}) collective-permute-start(bf16[256,4096]{1,0:T(8,128)(2,1)} %constant_dynamic-slice_fusion), channel_id=1, source_target_pairs={{0,2},{2,0},{1,3},{3,1},{4,6},{6,4},{5,7},{7,5},{8,10},{10,8},{9,1... | collective-permute-start | bytes 6291464 | tf_op jit(solution)/shard_map/ppermute | solution.py:232
  18.3 3.0 %fold.4 = (f32[4,512,128]{2,1,0:T(8,128)S(1)}, f32[4,512,256]{2,1,0:T(8,128)S(1)}, f32[4,256,128]{2,1,0:T(8,128)S(1)}, f32[4,256,256]{2,1,0:T(8,128)S(1)}) custom-call(bf16[512,512]{1,0:T(8,128)(2,1)S(1)} %get-tuple-element.35.q_ref, bf16[256,512]{1,0:T(8,128)(2,1)S(1)} %get-tuple-element.36.cq_ref, f32[256,128]{1,0:T(8,128)S(1)} %get-tuple-element.37.level_ref, ...), custom_call_target="tpu_custom_call" | custom-call | flops 1879048192 | bytes 262144 | tf_op jit(solution)/shard_map/fold/pallas_call | solution.py:146
  21.3 4.3 %collective-permute-done.5.refs_2_ = bf16[2,784,128]{2,1,0:T(8,128)(2,1)} collective-permute-done((bf16[2,784,128]{2,1,0:T(8,128)(2,1)S(1)}, bf16[2,784,128]{2,1,0:T(8,128)(2,1)}, u32[]{:S(2)}, u32[]{:S(2)}) %collective-permute-start.5) | collective-permute-done | bytes 401440 | tf_op jit(solution)/shard_map/ppermute | solution.py:241
  25.6 0.5 collective-permute-start.7
  26.6 0.9 slice.27
  27.5 5.0 %collective-permute-start.9 = (bf16[1,784,128]{2,1,0:T(8,128)(2,1)S(1)}, bf16[1,784,128]{2,1,0:T(8,128)(2,1)S(1)}, u32[]{:S(2)}, u32[]{:S(2)}) collective-permute-start(bf16[1,784,128]{2,1,0:T(8,128)(2,1)S(1)} %slice.27), channel_id=1, source_target_pairs={{0,32},{8,104},{16,48},{24,120},{32,64},{40,8},{48,80},{56,24},{64... | collective-permute-start | bytes 602120 | tf_op jit(solution)/shard_map/ppermute | solution.py:241
  32.5 11.7 %fold.5 = (f32[4,512,128]{2,1,0:T(8,128)S(1)}, f32[4,512,256]{2,1,0:T(8,128)S(1)}, f32[4,256,128]{2,1,0:T(8,128)S(1)}, f32[4,256,256]{2,1,0:T(8,128)S(1)}) custom-call(bf16[512,512]{1,0:T(8,128)(2,1)S(1)} %get-tuple-element.35.q_ref, ...), custom_call_target="tpu_custom_call", output_to_operand_aliasing={{0}: (7, {}), {1}: (8, {}), {2}: (9, {}), {3}: (10, {})} | custom-call | flops 7516192768 | bytes 262144 | tf_op jit(solution)/shard_map/fold/pallas_call | solution.py:146
  44.8 1.5 %collective-permute-done.11.refs_3_ = bf16[1,784,128]{2,1,0:T(8,128)(2,1)S(1)} collective-permute-done((bf16[1,784,128]{2,1,0:T(8,128)(2,1)S(1)}, bf16[1,784,128]{2,1,0:T(8,128)(2,1)S(1)}, u32[]{:S(2)}, u32[]{:S(2)}) %collective-permute-start.11) | collective-permute-done | bytes 200736 | tf_op jit(solution)/shard_map/ppermute | solution.py:232
  46.3 4.5 %fold.6 = (bf16[192,640]{1,0:T(8,128)(2,1)S(1)}, bf16[192,640]{1,0:T(8,128)(2,1)S(1)}) custom-call(bf16[512,512]{1,0:T(8,128)(2,1)S(1)} %get-tuple-element.35.q_ref, bf16[256,512]{1,0:T(8,128)(2,1)S(1)} %get-tuple-element.36.cq_ref, f32[256,128]{1,0:T(8,128)S(1)} %get-tuple-element.37.level_ref, bf16[2,784,128]{2,1,0:T(8,128)(2,1)S(1)} %collective-permute-done.8.refs_0_, ...), custom_call_target="tpu_custom_call" | custom-call | flops 5637144576 | bytes 262144 | tf_op jit(solution)/shard_map/fold/pallas_call | solution.py:146
  50.8 13.0 %collective-permute-done.w_mine = bf16[256,4096]{1,0:T(8,128)(2,1)S(1)} collective-permute-done((bf16[256,4096]{1,0:T(8,128)(2,1)}, bf16[256,4096]{1,0:T(8,128)(2,1)S(1)}, u32[]{:S(2)}, u32[]{:S(2)}) %collective-permute-start) | collective-permute-done | bytes 2097184 | tf_op jit(solution)/shard_map/ppermute | solution.py:232
  63.8 5.2 %fold.7 = (bf16[192,640]{1,0:T(8,128)(2,1)}, bf16[192,640]{1,0:T(8,128)(2,1)}) custom-call(bf16[512,512]{1,0:T(8,128)(2,1)S(1)} %get-tuple-element.35.q_ref, bf16[256,512]{1,0:T(8,128)(2,1)S(1)} %get-tuple-element.36.cq_ref, f32[256,128]{1,0:T(8,128)S(1)} %get-tuple-element.37.level_ref, bf16[2,784,128]{2,1,0:T(8,128)(2,1)S(1)} %collective-permute-done.8.refs_0_, ...), custom_call_target="tpu_custom_call" | custom-call | flops 5637144576 | bytes 262144 | tf_op jit(solution)/shard_map/fold/pallas_call | solution.py:146
  69.1 1.6 %collective-permute-start.12 = (bf16[192,640]{1,0:T(8,128)(2,1)}, bf16[192,640]{1,0:T(8,128)(2,1)S(1)}, u32[]{:S(2)}, u32[]{:S(2)}) collective-permute-start(bf16[192,640]{1,0:T(8,128)(2,1)} %get-tuple-element.60), channel_id=1, source_target_pairs={{0,128},{128,0},{1,129},{129,1},{2,130},{130,2},{3,131},{131,3},{4... | collective-permute-start | bytes 737288 | tf_op jit(solution)/shard_map/ppermute | solution.py:232
  70.7 2.9 %collective-permute-start.14 = (bf16[192,640]{1,0:T(8,128)(2,1)}, bf16[192,640]{1,0:T(8,128)(2,1)S(1)}, u32[]{:S(2)}, u32[]{:S(2)}) collective-permute-start(bf16[192,640]{1,0:T(8,128)(2,1)} %get-tuple-element.62), channel_id=1, source_target_pairs={{0,130},{2,128},{128,2},{130,0},{1,131},{3,129},{129,3},{131,1},{4... | collective-permute-start | bytes 737288 | tf_op jit(solution)/shard_map/ppermute | solution.py:232
  73.5 0.5 collective-permute-start.13
  74.1 8.8 %collective-permute-done.12.near = bf16[192,640]{1,0:T(8,128)(2,1)S(1)} collective-permute-done((bf16[192,640]{1,0:T(8,128)(2,1)}, bf16[192,640]{1,0:T(8,128)(2,1)S(1)}, u32[]{:S(2)}, u32[]{:S(2)}) %collective-permute-start.12) | collective-permute-done | bytes 245792 | tf_op jit(solution)/shard_map/ppermute | solution.py:232
  82.9 2.7 %collective-permute-done.13.cross = bf16[192,640]{1,0:T(8,128)(2,1)S(1)} collective-permute-done((bf16[192,640]{1,0:T(8,128)(2,1)S(1)}, bf16[192,640]{1,0:T(8,128)(2,1)S(1)}, u32[]{:S(2)}, u32[]{:S(2)}) %collective-permute-start.13) | collective-permute-done | bytes 245792 | tf_op jit(solution)/shard_map/ppermute | solution.py:232
  85.6 2.2 %copy-done = bf16[512,4096]{1,0:T(8,128)(2,1)S(1)} copy-done((bf16[512,4096]{1,0:T(8,128)(2,1)S(1)}, bf16[512,4096]{1,0:T(8,128)(2,1)}, u32[]{:S(2)}) %copy-start) | copy-done | bytes 4194328
  87.8 5.5 %project.1 = (bf16[48,4096]{1,0:T(8,128)(2,1)S(1)}, bf16[48,4096]{1,0:T(8,128)(2,1)S(1)}, bf16[48,4096]{1,0:T(8,128)(2,1)S(1)}, bf16[48,4096]{1,0:T(8,128)(2,1)S(1)}) custom-call(s32[2]{0:T(128)S(1)} %pad_add_fusion.place_ref, bf16[192,640]{1,0:T(8,128)(2,1)S(1)} %get-tuple-element.59.keep, bf16[192,640]{1,0:T(8,128)(2,1)S(1)} %collective-permute-done.12.near, ...), custom_call_target="tpu_custom_call" | custom-call | flops 1610612736 | bytes 8388608 | tf_op jit(solution)/shard_map/project/pallas_call | solution.py:213
  93.4 1.6 %collective-permute-start.16 = (bf16[48,4096]{1,0:T(8,128)(2,1)S(1)}, bf16[48,4096]{1,0:T(8,128)(2,1)S(1)}, u32[]{:S(2)}, u32[]{:S(2)}) collective-permute-start(bf16[48,4096]{1,0:T(8,128)(2,1)S(1)} %get-tuple-element.65), channel_id=1, source_target_pairs={{0,1},{1,0},{2,3},{3,2},{4,5},{5,4},{6,7},{7,6},{8,9},{9,8},{10,11... | collective-permute-start | bytes 1179656 | tf_op jit(solution)/shard_map/ppermute | solution.py:232
  94.9 3.2 %collective-permute-start.17 = (bf16[48,4096]{1,0:T(8,128)(2,1)S(1)}, bf16[48,4096]{1,0:T(8,128)(2,1)S(1)}, u32[]{:S(2)}, u32[]{:S(2)}) collective-permute-start(bf16[48,4096]{1,0:T(8,128)(2,1)S(1)} %get-tuple-element.66), channel_id=1, source_target_pairs={{0,4},{4,0},{1,5},{5,1},{2,6},{6,2},{3,7},{7,3},{8,12},{12,8},{9,1... | collective-permute-start | bytes 1179656 | tf_op jit(solution)/shard_map/ppermute | solution.py:232
  98.4 7.1 %collective-permute-done.16 = bf16[48,4096]{1,0:T(8,128)(2,1)S(1)} collective-permute-done((bf16[48,4096]{1,0:T(8,128)(2,1)S(1)}, bf16[48,4096]{1,0:T(8,128)(2,1)S(1)}, u32[]{:S(2)}, u32[]{:S(2)}) %collective-permute-start.16) | collective-permute-done | bytes 393248 | tf_op jit(solution)/shard_map/ppermute | solution.py:232
  105.5 8.7 %collective-permute-done.17 = bf16[48,4096]{1,0:T(8,128)(2,1)S(1)} collective-permute-done((bf16[48,4096]{1,0:T(8,128)(2,1)S(1)}, bf16[48,4096]{1,0:T(8,128)(2,1)S(1)}, u32[]{:S(2)}, u32[]{:S(2)}) %collective-permute-start.17) | collective-permute-done | bytes 393248 | tf_op jit(solution)/shard_map/ppermute | solution.py:232
  114.2 0.8 collective-permute-done.18
  115.0 0.7 add_convert_fusion.1
  115.7 0.8 add_convert_fusion
  (27 shorter events, 2.2 us)
Async XLA Ops:
  2.3 3.2 %collective-permute-start.3 = (bf16[784,128]{1,0:T(8,128)(2,1)S(1)}, bf16[784,128]{1,0:T(8,128)(2,1)S(1)}, u32[]{:S(2)}, u32[]{:S(2)}) collective-permute-start(bf16[784,128]{1,0:T(8,128)(2,1)S(1)} %get-tuple-element.69), channel_id=1, source_target_pairs={{0,8},{8,0},{1,9},{9,1},{2,10},{10,2},{3,11},{11,3},{4,12},{12,4},... | collective-permute-start | bytes 602120 | tf_op jit(solution)/shard_map/ppermute | solution.py:232
  3.4 14.8 %collective-permute-start.2 = (bf16[128,640]{1,0:T(8,128)(2,1)S(1)}, bf16[128,640]{1,0:T(8,128)(2,1)S(1)}, u32[]{:S(2)}, u32[]{:S(2)}) collective-permute-start(bf16[128,640]{1,0:T(8,128)(2,1)S(1)} %pad_maximum_fusion.2.coarse_mine), channel_id=1, source_target_pairs={{0,128},{128,0},{1,129},{129,1},{2,130},{130,2},{3,131},{131,3},{4... | collective-permute-start | bytes 491528 | tf_op jit(solution)/shard_map/ppermute | solution.py:232
  5.1 13.2 %collective-permute-start.1 = (bf16[256,512]{1,0:T(8,128)(2,1)}, bf16[256,512]{1,0:T(8,128)(2,1)S(1)}, u32[]{:S(2)}, u32[]{:S(2)}) collective-permute-start(bf16[256,512]{1,0:T(8,128)(2,1)} %fine_mine.1), channel_id=1, source_target_pairs={{0,128},{128,0},{1,129},{129,1},{2,130},{130,2},{3,131},{131,3},{4... | collective-permute-start | bytes 786440 | tf_op jit(solution)/shard_map/ppermute | solution.py:232
  5.6 12.7 %copy-start.1 = (bf16[256,512]{1,0:T(8,128)(2,1)S(1)}, bf16[256,512]{1,0:T(8,128)(2,1)}, u32[]{:S(2)}) copy-start(bf16[256,512]{1,0:T(8,128)(2,1)} %fine_mine.1) | copy-start | bytes 786436
  5.6 15.7 %collective-permute-start.4 = (bf16[2,784,128]{2,1,0:T(8,128)(2,1)S(1)}, bf16[2,784,128]{2,1,0:T(8,128)(2,1)}, u32[]{:S(2)}, u32[]{:S(2)}) collective-permute-start(bf16[2,784,128]{2,1,0:T(8,128)(2,1)S(1)} %pad_maximum_fusion.refs_0_), channel_id=1, source_target_pairs={{0,16},{8,120},{16,32},{24,8},{32,48},{40,24},{48,64},{56,40},{64,... | collective-permute-start | bytes 1204232 | tf_op jit(solution)/shard_map/ppermute | solution.py:241
  7.6 18.0 %collective-permute-start.5 = (bf16[2,784,128]{2,1,0:T(8,128)(2,1)S(1)}, bf16[2,784,128]{2,1,0:T(8,128)(2,1)}, u32[]{:S(2)}, u32[]{:S(2)}) collective-permute-start(bf16[2,784,128]{2,1,0:T(8,128)(2,1)S(1)} %pad_maximum_fusion.refs_0_), channel_id=1, source_target_pairs={{0,32},{8,104},{16,48},{24,120},{32,64},{40,8},{48,80},{56,24},{64... | collective-permute-start | bytes 1204232 | tf_op jit(solution)/shard_map/ppermute | solution.py:241
  15.2 48.6 %collective-permute-start = (bf16[256,4096]{1,0:T(8,128)(2,1)}, bf16[256,4096]{1,0:T(8,128)(2,1)S(1)}, u32[]{:S(2)}, u32[]{:S(2)}) collective-permute-start(bf16[256,4096]{1,0:T(8,128)(2,1)} %constant_dynamic-slice_fusion), channel_id=1, source_target_pairs={{0,2},{2,0},{1,3},{3,1},{4,6},{6,4},{5,7},{7,5},{8,10},{10,8},{9,1... | collective-permute-start | bytes 6291464 | tf_op jit(solution)/shard_map/ppermute | solution.py:232
  25.6 6.8 %collective-permute-start.6 = (bf16[2,784,128]{2,1,0:T(8,128)(2,1)}, bf16[2,784,128]{2,1,0:T(8,128)(2,1)S(1)}, u32[]{:S(2)}, u32[]{:S(2)}) collective-permute-start(bf16[2,784,128]{2,1,0:T(8,128)(2,1)} %collective-permute-done.4.refs_0_), channel_id=1, source_target_pairs={{0,8},{8,0},{1,9},{9,1},{2,10},{10,2},{3,11},{11,3},{4,12},{12,4},... | collective-permute-start | bytes 1204232 | tf_op jit(solution)/shard_map/ppermute | solution.py:232
  25.6 6.8 %collective-permute-start.7 = (bf16[2,784,128]{2,1,0:T(8,128)(2,1)}, bf16[2,784,128]{2,1,0:T(8,128)(2,1)S(1)}, u32[]{:S(2)}, u32[]{:S(2)}) collective-permute-start(bf16[2,784,128]{2,1,0:T(8,128)(2,1)} %collective-permute-done.5.refs_2_), channel_id=1, source_target_pairs={{0,8},{8,0},{1,9},{9,1},{2,10},{10,2},{3,11},{11,3},{4,12},{12,4},... | collective-permute-start | bytes 1204232 | tf_op jit(solution)/shard_map/ppermute | solution.py:232
  26.1 18.1 %collective-permute-start.8 = (bf16[2,784,128]{2,1,0:T(8,128)(2,1)}, bf16[2,784,128]{2,1,0:T(8,128)(2,1)S(1)}, u32[]{:S(2)}, u32[]{:S(2)}) collective-permute-start(bf16[2,784,128]{2,1,0:T(8,128)(2,1)} %collective-permute-done.4.refs_0_), channel_id=1, source_target_pairs={{0,32},{8,104},{16,48},{24,120},{32,64},{40,8},{48,80},{56,24},{64... | collective-permute-start | bytes 1204232 | tf_op jit(solution)/shard_map/ppermute | solution.py:241
  27.5 16.7 %collective-permute-start.9 = (bf16[1,784,128]{2,1,0:T(8,128)(2,1)S(1)}, bf16[1,784,128]{2,1,0:T(8,128)(2,1)S(1)}, u32[]{:S(2)}, u32[]{:S(2)}) collective-permute-start(bf16[1,784,128]{2,1,0:T(8,128)(2,1)S(1)} %slice.27), channel_id=1, source_target_pairs={{0,32},{8,104},{16,48},{24,120},{32,64},{40,8},{48,80},{56,24},{64... | collective-permute-start | bytes 602120 | tf_op jit(solution)/shard_map/ppermute | solution.py:241
  44.2 2.1 %collective-permute-start.10 = (bf16[2,784,128]{2,1,0:T(8,128)(2,1)S(1)}, bf16[2,784,128]{2,1,0:T(8,128)(2,1)S(1)}, u32[]{:S(2)}, u32[]{:S(2)}) collective-permute-start(bf16[2,784,128]{2,1,0:T(8,128)(2,1)S(1)} %collective-permute-done.8.refs_0_), channel_id=1, source_target_pairs={{0,8},{8,0},{1,9},{9,1},{2,10},{10,2},{3,11},{11,3},{4,12},{12,4},... | collective-permute-start | bytes 1204232 | tf_op jit(solution)/shard_map/ppermute | solution.py:232
  44.3 2.0 %collective-permute-start.11 = (bf16[1,784,128]{2,1,0:T(8,128)(2,1)S(1)}, bf16[1,784,128]{2,1,0:T(8,128)(2,1)S(1)}, u32[]{:S(2)}, u32[]{:S(2)}) collective-permute-start(bf16[1,784,128]{2,1,0:T(8,128)(2,1)S(1)} %collective-permute-done.9.refs_2_), channel_id=1, source_target_pairs={{0,8},{8,0},{1,9},{9,1},{2,10},{10,2},{3,11},{11,3},{4,12},{12,4},... | collective-permute-start | bytes 602120 | tf_op jit(solution)/shard_map/ppermute | solution.py:232
  63.8 21.8 %collective-permute-start.15 = (bf16[256,4096]{1,0:T(8,128)(2,1)S(1)}, bf16[256,4096]{1,0:T(8,128)(2,1)}, u32[]{:S(2)}, u32[]{:S(2)}) collective-permute-start(bf16[256,4096]{1,0:T(8,128)(2,1)S(1)} %collective-permute-done.w_mine), channel_id=1, source_target_pairs={{0,8},{8,0},{1,9},{9,1},{2,10},{10,2},{3,11},{11,3},{4,12},{12,4},... | collective-permute-start | bytes 6291464 | tf_op jit(solution)/shard_map/ppermute | solution.py:232
  69.1 13.8 %collective-permute-start.12 = (bf16[192,640]{1,0:T(8,128)(2,1)}, bf16[192,640]{1,0:T(8,128)(2,1)S(1)}, u32[]{:S(2)}, u32[]{:S(2)}) collective-permute-start(bf16[192,640]{1,0:T(8,128)(2,1)} %get-tuple-element.60), channel_id=1, source_target_pairs={{0,128},{128,0},{1,129},{129,1},{2,130},{130,2},{3,131},{131,3},{4... | collective-permute-start | bytes 737288 | tf_op jit(solution)/shard_map/ppermute | solution.py:232
  70.7 12.3 %collective-permute-start.14 = (bf16[192,640]{1,0:T(8,128)(2,1)}, bf16[192,640]{1,0:T(8,128)(2,1)S(1)}, u32[]{:S(2)}, u32[]{:S(2)}) collective-permute-start(bf16[192,640]{1,0:T(8,128)(2,1)} %get-tuple-element.62), channel_id=1, source_target_pairs={{0,130},{2,128},{128,2},{130,0},{1,131},{3,129},{129,3},{131,1},{4... | collective-permute-start | bytes 737288 | tf_op jit(solution)/shard_map/ppermute | solution.py:232
  73.5 12.1 %collective-permute-start.13 = (bf16[192,640]{1,0:T(8,128)(2,1)S(1)}, bf16[192,640]{1,0:T(8,128)(2,1)S(1)}, u32[]{:S(2)}, u32[]{:S(2)}) collective-permute-start(bf16[192,640]{1,0:T(8,128)(2,1)S(1)} %get-tuple-element.61), channel_id=1, source_target_pairs={{0,2},{2,0},{1,3},{3,1},{4,6},{6,4},{5,7},{7,5},{8,10},{10,8},{9,1... | collective-permute-start | bytes 737288 | tf_op jit(solution)/shard_map/ppermute | solution.py:232
  85.6 2.2 %copy-start = (bf16[512,4096]{1,0:T(8,128)(2,1)S(1)}, bf16[512,4096]{1,0:T(8,128)(2,1)}, u32[]{:S(2)}) copy-start(bf16[512,4096]{1,0:T(8,128)(2,1)} %w.1) | copy-start | bytes 12582916
  93.4 12.1 %collective-permute-start.16 = (bf16[48,4096]{1,0:T(8,128)(2,1)S(1)}, bf16[48,4096]{1,0:T(8,128)(2,1)S(1)}, u32[]{:S(2)}, u32[]{:S(2)}) collective-permute-start(bf16[48,4096]{1,0:T(8,128)(2,1)S(1)} %get-tuple-element.65), channel_id=1, source_target_pairs={{0,1},{1,0},{2,3},{3,2},{4,5},{5,4},{6,7},{7,6},{8,9},{9,8},{10,11... | collective-permute-start | bytes 1179656 | tf_op jit(solution)/shard_map/ppermute | solution.py:232
  94.9 19.2 %collective-permute-start.17 = (bf16[48,4096]{1,0:T(8,128)(2,1)S(1)}, bf16[48,4096]{1,0:T(8,128)(2,1)S(1)}, u32[]{:S(2)}, u32[]{:S(2)}) collective-permute-start(bf16[48,4096]{1,0:T(8,128)(2,1)S(1)} %get-tuple-element.66), channel_id=1, source_target_pairs={{0,4},{4,0},{1,5},{5,1},{2,6},{6,2},{3,7},{7,3},{8,12},{12,8},{9,1... | collective-permute-start | bytes 1179656 | tf_op jit(solution)/shard_map/ppermute | solution.py:232
  98.1 16.8 %collective-permute-start.18 = (bf16[48,4096]{1,0:T(8,128)(2,1)S(1)}, bf16[48,4096]{1,0:T(8,128)(2,1)S(1)}, u32[]{:S(2)}, u32[]{:S(2)}) collective-permute-start(bf16[48,4096]{1,0:T(8,128)(2,1)S(1)} %get-tuple-element.67), channel_id=1, source_target_pairs={{0,5},{1,4},{4,1},{5,0},{2,7},{3,6},{6,3},{7,2},{8,13},{9,12},{12,... | collective-permute-start | bytes 1179656 | tf_op jit(solution)/shard_map/ppermute | solution.py:232

commit v2 on v1

--- a/solution.py
+++ b/solution.py
@@ -151,7 +151,7 @@
         input_output_aliases=aliases,
         compiler_params=pltpu.CompilerParams(vmem_limit_bytes=GRANT),
         cost_estimate=pl.CostEstimate(
-            flops=8 * work * HD, bytes_accessed=q.size, transcendentals=0
+            flops=(1 if last else 8) * work * HD, bytes_accessed=q.size, transcendentals=0
         ),
         name="fold",
     )(*ins)
@@ -281,6 +281,22 @@
     )(xp, *arrays)
 
 
+def after_kernel(*refs):
+    pltpu.touch(refs[-1])
+
+
+def after(x, before):
+    return pl.pallas_call(
+        after_kernel,
+        out_shape=jax.ShapeDtypeStruct(x.shape, x.dtype),
+        in_specs=[pl.BlockSpec(memory_space=pl.ANY)] * (1 + len(before)),
+        out_specs=pl.BlockSpec(memory_space=pl.ANY),
+        input_output_aliases={0: 0},
+        compiler_params=pltpu.CompilerParams(vmem_limit_bytes=1 << 20),
+        name="after",
+    )(x, *before)
+
+
 def per_device(fine_query, fine_memory, coarse_query, coarse_memory, coarse_scale, out_weight):
     fine, coarse = fine_query.shape[0], coarse_query.shape[0]
     width = fine_query.shape[1]
@@ -322,7 +338,7 @@
     near, far = crossed(to_yl, ("yl",)), crossed(to_both, ("yl", "xp"))
     keep, to_xp = folded(blocks, state, 0)
     across = crossed(to_xp, ("xp",))
-    weight_mine, keep = lax.optimization_barrier((weight_mine, keep))
+    weight_mine = after(weight_mine, (near, far, across))
     weight_other = crossed(weight_mine, ("c",))
     shares = project(
         jnp.stack([core, lax.axis_index((HEAD[0], HEAD[2]))]),

time: 117 us -> 111 us (0.949)
  waiting for transfers between devices: 47 us -> 41.1 us
    ppermute x15, waiting for transfers between devices: 42.6 us -> 36.8 us  [crossed(): return lax.ppermute(x, axes, [(i, n - 1 - i) for i in range(n)])]
  transfers between devices with their start and end apart: 19 -> 19, of which waited for: 8 -> 8; matrix products, arithmetic and copies ran while one was open for 4% -> 5% of each run, Pallas kernels for 21% -> 22%
where the time goes in v2:
time: 111 us; the launch traced here: 110 us
  waiting for transfers between devices  41.1 us (37%)
  Pallas kernels  29.4 us (26%)
  starting transfers between devices  28.4 us (26%)
  local copies, waits for them, and re-layouts  6.36 us (6%)
  other arithmetic  4.25 us (4%)
    ppermute x15, waiting for transfers between devices, crossed(): return lax.ppermute(x, axes, [(i, n - 1 - i) for i in range(n)])  36.8 us
    pallas_call x4, Pallas kernels, fold(): pl.pallas_call(functools.partial(fold_kernel, len(blocks), fine, coarse,...  23.8 us
    ppermute x15, starting transfers between devices, crossed(): return lax.ppermute(x, axes, [(i, n - 1 - i) for i in range(n)])  16.6 us
    ppermute x4, starting transfers between devices, along_z(): return lax.ppermute(x, ('z', 'c'), pairs)  11.9 us
    pallas_call x1, Pallas kernels, project(): pl.pallas_call(functools.partial(project_kernel, n_fine, n_blocks), grid=...  5.52 us
    ppermute x4, waiting for transfers between devices, along_z(): return lax.ppermute(x, ('z', 'c'), pairs)  4.34 us
    dynamic_slice x1, local copies, waits for them, and re-layouts, per_device(): lax.dynamic_slice_in_dim(out_weight, core * depth, depth, 0)  3.14 us
  transfers between devices with their start and end apart: 19, of which 8 were waited for; matrix products, arithmetic and copies ran while one was open for 5% of the time, Pallas kernels for 22%

profile of v2, /device:TPU:32, one launch (start us, length us, event | category | flops | bytes accessed | tf_op | source)
XLA Modules:
  0.0 110.3 jit_solution(9428690988375994980)
XLA Ops:
  0.6 0.7 convert_element_type.33
  1.3 1.0 fusion
  2.5 0.9 pad_maximum_fusion.2.coarse_mine
  3.4 1.7 %collective-permute-start.1 = (bf16[128,640]{1,0:T(8,128)(2,1)S(1)}, bf16[128,640]{1,0:T(8,128)(2,1)S(1)}, u32[]{:S(2)}, u32[]{:S(2)}) collective-permute-start(bf16[128,640]{1,0:T(8,128)(2,1)S(1)} %pad_maximum_fusion.2.coarse_mine), channel_id=1, source_target_pairs={{0,128},{128,0},{1,129},{129,1},{2,130},{130,2},{3,131},{131,3},{4... | collective-permute-start | bytes 491528 | tf_op jit(solution)/shard_map/ppermute | solution.py:232
  5.6 2.0 %collective-permute-start.3 = (bf16[2,784,128]{2,1,0:T(8,128)(2,1)S(1)}, bf16[2,784,128]{2,1,0:T(8,128)(2,1)}, u32[]{:S(2)}, u32[]{:S(2)}) collective-permute-start(bf16[2,784,128]{2,1,0:T(8,128)(2,1)S(1)} %pad_maximum_fusion.refs_0_), channel_id=1, source_target_pairs={{0,16},{8,120},{16,32},{24,8},{32,48},{40,24},{48,64},{56,40},{64,... | collective-permute-start | bytes 1204232 | tf_op jit(solution)/shard_map/ppermute | solution.py:241
  7.6 4.5 %collective-permute-start.4 = (bf16[2,784,128]{2,1,0:T(8,128)(2,1)S(1)}, bf16[2,784,128]{2,1,0:T(8,128)(2,1)}, u32[]{:S(2)}, u32[]{:S(2)}) collective-permute-start(bf16[2,784,128]{2,1,0:T(8,128)(2,1)S(1)} %pad_maximum_fusion.refs_0_), channel_id=1, source_target_pairs={{0,32},{8,104},{16,48},{24,120},{32,64},{40,8},{48,80},{56,24},{64... | collective-permute-start | bytes 1204232 | tf_op jit(solution)/shard_map/ppermute | solution.py:241
  12.1 3.1 %constant_dynamic-slice_fusion = bf16[256,4096]{1,0:T(8,128)(2,1)} fusion(bf16[512,4096]{1,0:T(8,128)(2,1)} %w.1, s32[]{:T(128)S(6)} %select_n.3), kind=kLoop, calls=%fused_computation.6 | loop fusion | bytes 4194308 | tf_op jit(solution)/shard_map/dynamic_slice | solution.py:319
  15.2 3.0 %collective-permute-start.14 = (bf16[256,4096]{1,0:T(8,128)(2,1)}, bf16[256,4096]{1,0:T(8,128)(2,1)S(1)}, u32[]{:S(2)}, u32[]{:S(2)}) collective-permute-start(bf16[256,4096]{1,0:T(8,128)(2,1)} %constant_dynamic-slice_fusion), channel_id=1, source_target_pairs={{0,2},{2,0},{1,3},{3,1},{4,6},{6,4},{5,7},{7,5},{8,10},{10,8},{9,1... | collective-permute-start | bytes 6291464 | tf_op jit(solution)/shard_map/ppermute | solution.py:232
  18.3 3.0 %fold.4 = (f32[4,512,128]{2,1,0:T(8,128)S(1)}, f32[4,512,256]{2,1,0:T(8,128)S(1)}, f32[4,256,128]{2,1,0:T(8,128)S(1)}, f32[4,256,256]{2,1,0:T(8,128)S(1)}) custom-call(bf16[512,512]{1,0:T(8,128)(2,1)S(1)} %get-tuple-element.33.q_ref, bf16[256,512]{1,0:T(8,128)(2,1)S(1)} %get-tuple-element.34.cq_ref, f32[256,128]{1,0:T(8,128)S(1)} %get-tuple-element.35.level_ref, ...), custom_call_target="tpu_custom_call" | custom-call | flops 1879048192 | bytes 262144 | tf_op jit(solution)/shard_map/fold/pallas_call | solution.py:146
  21.3 4.3 %collective-permute-done.4.refs_2_ = bf16[2,784,128]{2,1,0:T(8,128)(2,1)} collective-permute-done((bf16[2,784,128]{2,1,0:T(8,128)(2,1)S(1)}, bf16[2,784,128]{2,1,0:T(8,128)(2,1)}, u32[]{:S(2)}, u32[]{:S(2)}) %collective-permute-start.4) | collective-permute-done | bytes 401440 | tf_op jit(solution)/shard_map/ppermute | solution.py:241
  25.6 0.5 collective-permute-start.6
  26.6 0.9 slice.27
  27.5 5.0 %collective-permute-start.8 = (bf16[1,784,128]{2,1,0:T(8,128)(2,1)S(1)}, bf16[1,784,128]{2,1,0:T(8,128)(2,1)S(1)}, u32[]{:S(2)}, u32[]{:S(2)}) collective-permute-start(bf16[1,784,128]{2,1,0:T(8,128)(2,1)S(1)} %slice.27), channel_id=1, source_target_pairs={{0,32},{8,104},{16,48},{24,120},{32,64},{40,8},{48,80},{56,24},{64... | collective-permute-start | bytes 602120 | tf_op jit(solution)/shard_map/ppermute | solution.py:241
  32.5 11.7 %fold.5 = (f32[4,512,128]{2,1,0:T(8,128)S(1)}, f32[4,512,256]{2,1,0:T(8,128)S(1)}, f32[4,256,128]{2,1,0:T(8,128)S(1)}, f32[4,256,256]{2,1,0:T(8,128)S(1)}) custom-call(bf16[512,512]{1,0:T(8,128)(2,1)S(1)} %get-tuple-element.33.q_ref, ...), custom_call_target="tpu_custom_call", output_to_operand_aliasing={{0}: (7, {}), {1}: (8, {}), {2}: (9, {}), {3}: (10, {})} | custom-call | flops 7516192768 | bytes 262144 | tf_op jit(solution)/shard_map/fold/pallas_call | solution.py:146
  44.8 1.5 %collective-permute-done.10.refs_3_ = bf16[1,784,128]{2,1,0:T(8,128)(2,1)S(1)} collective-permute-done((bf16[1,784,128]{2,1,0:T(8,128)(2,1)S(1)}, bf16[1,784,128]{2,1,0:T(8,128)(2,1)S(1)}, u32[]{:S(2)}, u32[]{:S(2)}) %collective-permute-start.10) | collective-permute-done | bytes 200736 | tf_op jit(solution)/shard_map/ppermute | solution.py:232
  46.3 4.5 %fold.7 = (bf16[192,640]{1,0:T(8,128)(2,1)S(1)}, bf16[192,640]{1,0:T(8,128)(2,1)S(1)}) custom-call(bf16[512,512]{1,0:T(8,128)(2,1)S(1)} %get-tuple-element.33.q_ref, bf16[256,512]{1,0:T(8,128)(2,1)S(1)} %get-tuple-element.34.cq_ref, f32[256,128]{1,0:T(8,128)S(1)} %get-tuple-element.35.level_ref, bf16[2,784,128]{2,1,0:T(8,128)(2,1)S(1)} %collective-permute-done.7.refs_0_, ...), custom_call_target="tpu_custom_call" | custom-call | flops 704643072 | bytes 262144 | tf_op jit(solution)/shard_map/fold/pallas_call | solution.py:146
  50.9 1.7 %collective-permute-start.11 = (bf16[192,640]{1,0:T(8,128)(2,1)S(1)}, bf16[192,640]{1,0:T(8,128)(2,1)S(1)}, u32[]{:S(2)}, u32[]{:S(2)}) collective-permute-start(bf16[192,640]{1,0:T(8,128)(2,1)S(1)} %get-tuple-element.57), channel_id=1, source_target_pairs={{0,128},{128,0},{1,129},{129,1},{2,130},{130,2},{3,131},{131,3},{4... | collective-permute-start | bytes 737288 | tf_op jit(solution)/shard_map/ppermute | solution.py:232
  52.5 2.9 %collective-permute-start.13 = (bf16[192,640]{1,0:T(8,128)(2,1)S(1)}, bf16[192,640]{1,0:T(8,128)(2,1)S(1)}, u32[]{:S(2)}, u32[]{:S(2)}) collective-permute-start(bf16[192,640]{1,0:T(8,128)(2,1)S(1)} %get-tuple-element.59), channel_id=1, source_target_pairs={{0,130},{2,128},{128,2},{130,0},{1,131},{3,129},{129,3},{131,1},{4... | collective-permute-start | bytes 737288 | tf_op jit(solution)/shard_map/ppermute | solution.py:232
  55.5 4.5 %fold.6 = (bf16[192,640]{1,0:T(8,128)(2,1)S(1)}, bf16[192,640]{1,0:T(8,128)(2,1)S(1)}) custom-call(bf16[512,512]{1,0:T(8,128)(2,1)S(1)} %get-tuple-element.33.q_ref, bf16[256,512]{1,0:T(8,128)(2,1)S(1)} %get-tuple-element.34.cq_ref, f32[256,128]{1,0:T(8,128)S(1)} %get-tuple-element.35.level_ref, bf16[2,784,128]{2,1,0:T(8,128)(2,1)S(1)} %collective-permute-done.7.refs_0_, ...), custom_call_target="tpu_custom_call" | custom-call | flops 704643072 | bytes 262144 | tf_op jit(solution)/shard_map/fold/pallas_call | solution.py:146
  60.0 0.6 collective-permute-start.12
  60.6 11.2 %collective-permute-done.13.refs_2_.far = bf16[192,640]{1,0:T(8,128)(2,1)S(1)} collective-permute-done((bf16[192,640]{1,0:T(8,128)(2,1)S(1)}, bf16[192,640]{1,0:T(8,128)(2,1)S(1)}, u32[]{:S(2)}, u32[]{:S(2)}) %collective-permute-start.13) | collective-permute-done | bytes 245792 | tf_op jit(solution)/shard_map/ppermute | solution.py:232
  71.8 2.6 %collective-permute-done.12.refs_3_.cross = bf16[192,640]{1,0:T(8,128)(2,1)S(1)} collective-permute-done((bf16[192,640]{1,0:T(8,128)(2,1)S(1)}, bf16[192,640]{1,0:T(8,128)(2,1)S(1)}, u32[]{:S(2)}, u32[]{:S(2)}) %collective-permute-start.12) | collective-permute-done | bytes 245792 | tf_op jit(solution)/shard_map/ppermute | solution.py:232
  74.5 4.2 %collective-permute-done.15.w_other = bf16[256,4096]{1,0:T(8,128)(2,1)} collective-permute-done((bf16[256,4096]{1,0:T(8,128)(2,1)S(1)}, bf16[256,4096]{1,0:T(8,128)(2,1)}, u32[]{:S(2)}, u32[]{:S(2)}) %collective-permute-start.15) | collective-permute-done | bytes 2097184 | tf_op jit(solution)/shard_map/ppermute | solution.py:232
  78.7 2.2 %copy-done = bf16[512,4096]{1,0:T(8,128)(2,1)S(1)} copy-done((bf16[512,4096]{1,0:T(8,128)(2,1)S(1)}, bf16[512,4096]{1,0:T(8,128)(2,1)}, u32[]{:S(2)}) %copy-start) | copy-done | bytes 4194328
  80.9 5.5 %project.1 = (bf16[48,4096]{1,0:T(8,128)(2,1)S(1)}, bf16[48,4096]{1,0:T(8,128)(2,1)S(1)}, bf16[48,4096]{1,0:T(8,128)(2,1)S(1)}, bf16[48,4096]{1,0:T(8,128)(2,1)S(1)}) custom-call(s32[2]{0:T(128)S(1)} %pad_add_fusion.place_ref, bf16[192,640]{1,0:T(8,128)(2,1)S(1)} %get-tuple-element.56.keep, bf16[192,640]{1,0:T(8,128)(2,1)S(1)} %collective-permute-done.11.refs_1_.near, ...), custom_call_target="tpu_custom_call" | custom-call | flops 1610612736 | bytes 8388608 | tf_op jit(solution)/shard_map/project/pallas_call | solution.py:213
  86.4 1.6 %collective-permute-start.16 = (bf16[48,4096]{1,0:T(8,128)(2,1)S(1)}, bf16[48,4096]{1,0:T(8,128)(2,1)S(1)}, u32[]{:S(2)}, u32[]{:S(2)}) collective-permute-start(bf16[48,4096]{1,0:T(8,128)(2,1)S(1)} %get-tuple-element.61), channel_id=1, source_target_pairs={{0,1},{1,0},{2,3},{3,2},{4,5},{5,4},{6,7},{7,6},{8,9},{9,8},{10,11... | collective-permute-start | bytes 1179656 | tf_op jit(solution)/shard_map/ppermute | solution.py:232
  88.0 3.2 %collective-permute-start.17 = (bf16[48,4096]{1,0:T(8,128)(2,1)S(1)}, bf16[48,4096]{1,0:T(8,128)(2,1)S(1)}, u32[]{:S(2)}, u32[]{:S(2)}) collective-permute-start(bf16[48,4096]{1,0:T(8,128)(2,1)S(1)} %get-tuple-element.62), channel_id=1, source_target_pairs={{0,4},{4,0},{1,5},{5,1},{2,6},{6,2},{3,7},{7,3},{8,12},{12,8},{9,1... | collective-permute-start | bytes 1179656 | tf_op jit(solution)/shard_map/ppermute | solution.py:232
  91.5 7.0 %collective-permute-done.16 = bf16[48,4096]{1,0:T(8,128)(2,1)S(1)} collective-permute-done((bf16[48,4096]{1,0:T(8,128)(2,1)S(1)}, bf16[48,4096]{1,0:T(8,128)(2,1)S(1)}, u32[]{:S(2)}, u32[]{:S(2)}) %collective-permute-start.16) | collective-permute-done | bytes 393248 | tf_op jit(solution)/shard_map/ppermute | solution.py:232
  98.4 9.6 %collective-permute-done.17 = bf16[48,4096]{1,0:T(8,128)(2,1)S(1)} collective-permute-done((bf16[48,4096]{1,0:T(8,128)(2,1)S(1)}, bf16[48,4096]{1,0:T(8,128)(2,1)S(1)}, u32[]{:S(2)}, u32[]{:S(2)}) %collective-permute-start.17) | collective-permute-done | bytes 393248 | tf_op jit(solution)/shard_map/ppermute | solution.py:232
  108.0 0.8 collective-permute-done.18
  108.8 0.7 add_convert_fusion.1
  109.5 0.8 add_convert_fusion
  (28 shorter events, 2.2 us)
Async XLA Ops:
  2.3 3.2 %collective-permute-start.2 = (bf16[784,128]{1,0:T(8,128)(2,1)S(1)}, bf16[784,128]{1,0:T(8,128)(2,1)S(1)}, u32[]{:S(2)}, u32[]{:S(2)}) collective-permute-start(bf16[784,128]{1,0:T(8,128)(2,1)S(1)} %get-tuple-element.65), channel_id=1, source_target_pairs={{0,8},{8,0},{1,9},{9,1},{2,10},{10,2},{3,11},{11,3},{4,12},{12,4},... | collective-permute-start | bytes 602120 | tf_op jit(solution)/shard_map/ppermute | solution.py:232
  3.4 14.8 %collective-permute-start.1 = (bf16[128,640]{1,0:T(8,128)(2,1)S(1)}, bf16[128,640]{1,0:T(8,128)(2,1)S(1)}, u32[]{:S(2)}, u32[]{:S(2)}) collective-permute-start(bf16[128,640]{1,0:T(8,128)(2,1)S(1)} %pad_maximum_fusion.2.coarse_mine), channel_id=1, source_target_pairs={{0,128},{128,0},{1,129},{129,1},{2,130},{130,2},{3,131},{131,3},{4... | collective-permute-start | bytes 491528 | tf_op jit(solution)/shard_map/ppermute | solution.py:232
  5.1 13.2 %collective-permute-start = (bf16[256,512]{1,0:T(8,128)(2,1)}, bf16[256,512]{1,0:T(8,128)(2,1)S(1)}, u32[]{:S(2)}, u32[]{:S(2)}) collective-permute-start(bf16[256,512]{1,0:T(8,128)(2,1)} %fine_mine.1), channel_id=1, source_target_pairs={{0,128},{128,0},{1,129},{129,1},{2,130},{130,2},{3,131},{131,3},{4... | collective-permute-start | bytes 786440 | tf_op jit(solution)/shard_map/ppermute | solution.py:232
  5.6 12.7 %copy-start.1 = (bf16[256,512]{1,0:T(8,128)(2,1)S(1)}, bf16[256,512]{1,0:T(8,128)(2,1)}, u32[]{:S(2)}) copy-start(bf16[256,512]{1,0:T(8,128)(2,1)} %fine_mine.1) | copy-start | bytes 786436
  5.6 15.7 %collective-permute-start.3 = (bf16[2,784,128]{2,1,0:T(8,128)(2,1)S(1)}, bf16[2,784,128]{2,1,0:T(8,128)(2,1)}, u32[]{:S(2)}, u32[]{:S(2)}) collective-permute-start(bf16[2,784,128]{2,1,0:T(8,128)(2,1)S(1)} %pad_maximum_fusion.refs_0_), channel_id=1, source_target_pairs={{0,16},{8,120},{16,32},{24,8},{32,48},{40,24},{48,64},{56,40},{64,... | collective-permute-start | bytes 1204232 | tf_op jit(solution)/shard_map/ppermute | solution.py:241
  7.6 18.0 %collective-permute-start.4 = (bf16[2,784,128]{2,1,0:T(8,128)(2,1)S(1)}, bf16[2,784,128]{2,1,0:T(8,128)(2,1)}, u32[]{:S(2)}, u32[]{:S(2)}) collective-permute-start(bf16[2,784,128]{2,1,0:T(8,128)(2,1)S(1)} %pad_maximum_fusion.refs_0_), channel_id=1, source_target_pairs={{0,32},{8,104},{16,48},{24,120},{32,64},{40,8},{48,80},{56,24},{64... | collective-permute-start | bytes 1204232 | tf_op jit(solution)/shard_map/ppermute | solution.py:241
  15.2 59.2 %collective-permute-start.14 = (bf16[256,4096]{1,0:T(8,128)(2,1)}, bf16[256,4096]{1,0:T(8,128)(2,1)S(1)}, u32[]{:S(2)}, u32[]{:S(2)}) collective-permute-start(bf16[256,4096]{1,0:T(8,128)(2,1)} %constant_dynamic-slice_fusion), channel_id=1, source_target_pairs={{0,2},{2,0},{1,3},{3,1},{4,6},{6,4},{5,7},{7,5},{8,10},{10,8},{9,1... | collective-permute-start | bytes 6291464 | tf_op jit(solution)/shard_map/ppermute | solution.py:232
  25.6 6.8 %collective-permute-start.5 = (bf16[2,784,128]{2,1,0:T(8,128)(2,1)}, bf16[2,784,128]{2,1,0:T(8,128)(2,1)S(1)}, u32[]{:S(2)}, u32[]{:S(2)}) collective-permute-start(bf16[2,784,128]{2,1,0:T(8,128)(2,1)} %collective-permute-done.3.refs_0_), channel_id=1, source_target_pairs={{0,8},{8,0},{1,9},{9,1},{2,10},{10,2},{3,11},{11,3},{4,12},{12,4},... | collective-permute-start | bytes 1204232 | tf_op jit(solution)/shard_map/ppermute | solution.py:232
  25.6 6.8 %collective-permute-start.6 = (bf16[2,784,128]{2,1,0:T(8,128)(2,1)}, bf16[2,784,128]{2,1,0:T(8,128)(2,1)S(1)}, u32[]{:S(2)}, u32[]{:S(2)}) collective-permute-start(bf16[2,784,128]{2,1,0:T(8,128)(2,1)} %collective-permute-done.4.refs_2_), channel_id=1, source_target_pairs={{0,8},{8,0},{1,9},{9,1},{2,10},{10,2},{3,11},{11,3},{4,12},{12,4},... | collective-permute-start | bytes 1204232 | tf_op jit(solution)/shard_map/ppermute | solution.py:232
  26.1 18.1 %collective-permute-start.7 = (bf16[2,784,128]{2,1,0:T(8,128)(2,1)}, bf16[2,784,128]{2,1,0:T(8,128)(2,1)S(1)}, u32[]{:S(2)}, u32[]{:S(2)}) collective-permute-start(bf16[2,784,128]{2,1,0:T(8,128)(2,1)} %collective-permute-done.3.refs_0_), channel_id=1, source_target_pairs={{0,32},{8,104},{16,48},{24,120},{32,64},{40,8},{48,80},{56,24},{64... | collective-permute-start | bytes 1204232 | tf_op jit(solution)/shard_map/ppermute | solution.py:241
  27.5 16.7 %collective-permute-start.8 = (bf16[1,784,128]{2,1,0:T(8,128)(2,1)S(1)}, bf16[1,784,128]{2,1,0:T(8,128)(2,1)S(1)}, u32[]{:S(2)}, u32[]{:S(2)}) collective-permute-start(bf16[1,784,128]{2,1,0:T(8,128)(2,1)S(1)} %slice.27), channel_id=1, source_target_pairs={{0,32},{8,104},{16,48},{24,120},{32,64},{40,8},{48,80},{56,24},{64... | collective-permute-start | bytes 602120 | tf_op jit(solution)/shard_map/ppermute | solution.py:241
  44.2 2.1 %collective-permute-start.9 = (bf16[2,784,128]{2,1,0:T(8,128)(2,1)S(1)}, bf16[2,784,128]{2,1,0:T(8,128)(2,1)S(1)}, u32[]{:S(2)}, u32[]{:S(2)}) collective-permute-start(bf16[2,784,128]{2,1,0:T(8,128)(2,1)S(1)} %collective-permute-done.7.refs_0_), channel_id=1, source_target_pairs={{0,8},{8,0},{1,9},{9,1},{2,10},{10,2},{3,11},{11,3},{4,12},{12,4},... | collective-permute-start | bytes 1204232 | tf_op jit(solution)/shard_map/ppermute | solution.py:232
  44.3 2.0 %collective-permute-start.10 = (bf16[1,784,128]{2,1,0:T(8,128)(2,1)S(1)}, bf16[1,784,128]{2,1,0:T(8,128)(2,1)S(1)}, u32[]{:S(2)}, u32[]{:S(2)}) collective-permute-start(bf16[1,784,128]{2,1,0:T(8,128)(2,1)S(1)} %collective-permute-done.8.refs_2_), channel_id=1, source_target_pairs={{0,8},{8,0},{1,9},{9,1},{2,10},{10,2},{3,11},{11,3},{4,12},{12,4},... | collective-permute-start | bytes 602120 | tf_op jit(solution)/shard_map/ppermute | solution.py:232
  50.9 9.7 %collective-permute-start.11 = (bf16[192,640]{1,0:T(8,128)(2,1)S(1)}, bf16[192,640]{1,0:T(8,128)(2,1)S(1)}, u32[]{:S(2)}, u32[]{:S(2)}) collective-permute-start(bf16[192,640]{1,0:T(8,128)(2,1)S(1)} %get-tuple-element.57), channel_id=1, source_target_pairs={{0,128},{128,0},{1,129},{129,1},{2,130},{130,2},{3,131},{131,3},{4... | collective-permute-start | bytes 737288 | tf_op jit(solution)/shard_map/ppermute | solution.py:232
  52.5 19.2 %collective-permute-start.13 = (bf16[192,640]{1,0:T(8,128)(2,1)S(1)}, bf16[192,640]{1,0:T(8,128)(2,1)S(1)}, u32[]{:S(2)}, u32[]{:S(2)}) collective-permute-start(bf16[192,640]{1,0:T(8,128)(2,1)S(1)} %get-tuple-element.59), channel_id=1, source_target_pairs={{0,130},{2,128},{128,2},{130,0},{1,131},{3,129},{129,3},{131,1},{4... | collective-permute-start | bytes 737288 | tf_op jit(solution)/shard_map/ppermute | solution.py:232
  60.0 14.4 %collective-permute-start.12 = (bf16[192,640]{1,0:T(8,128)(2,1)S(1)}, bf16[192,640]{1,0:T(8,128)(2,1)S(1)}, u32[]{:S(2)}, u32[]{:S(2)}) collective-permute-start(bf16[192,640]{1,0:T(8,128)(2,1)S(1)} %get-tuple-element.58), channel_id=1, source_target_pairs={{0,2},{2,0},{1,3},{3,1},{4,6},{6,4},{5,7},{7,5},{8,10},{10,8},{9,1... | collective-permute-start | bytes 737288 | tf_op jit(solution)/shard_map/ppermute | solution.py:232
  74.4 4.3 %collective-permute-start.15 = (bf16[256,4096]{1,0:T(8,128)(2,1)S(1)}, bf16[256,4096]{1,0:T(8,128)(2,1)}, u32[]{:S(2)}, u32[]{:S(2)}) collective-permute-start(bf16[256,4096]{1,0:T(8,128)(2,1)S(1)} %after.1.w_mine), channel_id=1, source_target_pairs={{0,8},{8,0},{1,9},{9,1},{2,10},{10,2},{3,11},{11,3},{4,12},{12,4},... | collective-permute-start | bytes 6291464 | tf_op jit(solution)/shard_map/ppermute | solution.py:232
  78.7 2.2 %copy-start = (bf16[512,4096]{1,0:T(8,128)(2,1)S(1)}, bf16[512,4096]{1,0:T(8,128)(2,1)}, u32[]{:S(2)}) copy-start(bf16[512,4096]{1,0:T(8,128)(2,1)} %w.1) | copy-start | bytes 12582916
  86.4 12.0 %collective-permute-start.16 = (bf16[48,4096]{1,0:T(8,128)(2,1)S(1)}, bf16[48,4096]{1,0:T(8,128)(2,1)S(1)}, u32[]{:S(2)}, u32[]{:S(2)}) collective-permute-start(bf16[48,4096]{1,0:T(8,128)(2,1)S(1)} %get-tuple-element.61), channel_id=1, source_target_pairs={{0,1},{1,0},{2,3},{3,2},{4,5},{5,4},{6,7},{7,6},{8,9},{9,8},{10,11... | collective-permute-start | bytes 1179656 | tf_op jit(solution)/shard_map/ppermute | solution.py:232
  88.0 20.0 %collective-permute-start.17 = (bf16[48,4096]{1,0:T(8,128)(2,1)S(1)}, bf16[48,4096]{1,0:T(8,128)(2,1)S(1)}, u32[]{:S(2)}, u32[]{:S(2)}) collective-permute-start(bf16[48,4096]{1,0:T(8,128)(2,1)S(1)} %get-tuple-element.62), channel_id=1, source_target_pairs={{0,4},{4,0},{1,5},{5,1},{2,6},{6,2},{3,7},{7,3},{8,12},{12,8},{9,1... | collective-permute-start | bytes 1179656 | tf_op jit(solution)/shard_map/ppermute | solution.py:232
  91.2 17.6 %collective-permute-start.18 = (bf16[48,4096]{1,0:T(8,128)(2,1)S(1)}, bf16[48,4096]{1,0:T(8,128)(2,1)S(1)}, u32[]{:S(2)}, u32[]{:S(2)}) collective-permute-start(bf16[48,4096]{1,0:T(8,128)(2,1)S(1)} %get-tuple-element.63), channel_id=1, source_target_pairs={{0,5},{1,4},{4,1},{5,0},{2,7},{3,6},{6,3},{7,2},{8,13},{9,12},{12,... | collective-permute-start | bytes 1179656 | tf_op jit(solution)/shard_map/ppermute | solution.py:232

commit v3 on v2

--- a/solution.py
+++ b/solution.py
@@ -151,7 +151,7 @@
         input_output_aliases=aliases,
         compiler_params=pltpu.CompilerParams(vmem_limit_bytes=GRANT),
         cost_estimate=pl.CostEstimate(
-            flops=(1 if last else 8) * work * HD, bytes_accessed=q.size, transcendentals=0
+            flops=(work if last else 8 * work * HD), bytes_accessed=q.size, transcendentals=0
         ),
         name="fold",
     )(*ins)

time: 111 us -> 108 us (0.973)
  waiting for transfers between devices: 41.1 us -> 38.9 us
    ppermute x15, waiting for transfers between devices: 36.8 us -> 34.3 us  [crossed(): return lax.ppermute(x, axes, [(i, n - 1 - i) for i in range(n)])]
  transfers between devices with their start and end apart: 19 -> 19, of which waited for: 8 -> 9; matrix products, arithmetic and copies ran while one was open for 5% -> 6% of each run, Pallas kernels for 22% -> 22%
where the time goes in v3:
time: 108 us; the launch traced here: 107 us
  waiting for transfers between devices  38.9 us (36%)
  Pallas kernels  29.4 us (27%)
  starting transfers between devices  28.5 us (26%)
  local copies, waits for them, and re-layouts  6.43 us (6%)
  other arithmetic  3.34 us (3%)
    ppermute x15, waiting for transfers between devices, crossed(): return lax.ppermute(x, axes, [(i, n - 1 - i) for i in range(n)])  34.3 us
    pallas_call x4, Pallas kernels, fold(): pl.pallas_call(functools.partial(fold_kernel, len(blocks), fine, coarse,...  23.8 us
    ppermute x15, starting transfers between devices, crossed(): return lax.ppermute(x, axes, [(i, n - 1 - i) for i in range(n)])  16.7 us
    ppermute x4, starting transfers between devices, along_z(): return lax.ppermute(x, ('z', 'c'), pairs)  11.9 us
    pallas_call x1, Pallas kernels, project(): pl.pallas_call(functools.partial(project_kernel, n_fine, n_blocks), grid=...  5.52 us
    ppermute x4, waiting for transfers between devices, along_z(): return lax.ppermute(x, ('z', 'c'), pairs)  4.57 us
    dynamic_slice x1, local copies, waits for them, and re-layouts, per_device(): lax.dynamic_slice_in_dim(out_weight, core * depth, depth, 0)  3.21 us
    unnamed x6, local copies, waits for them, and re-layouts  2.2 us
  transfers between devices with their start and end apart: 19, of which 9 were waited for; matrix products, arithmetic and copies ran while one was open for 6% of the time, Pallas kernels for 22%

profile of v3, /device:TPU:32, one launch (start us, length us, event | category | flops | bytes accessed | tf_op | source)
XLA Modules:
  0.0 107.3 jit_solution(7632967392333534509)
XLA Ops:
  0.6 1.7 %collective-permute-start = (bf16[256,512]{1,0:T(8,128)(2,1)}, bf16[256,512]{1,0:T(8,128)(2,1)S(1)}, u32[]{:S(2)}, u32[]{:S(2)}) collective-permute-start(bf16[256,512]{1,0:T(8,128)(2,1)} %fine_mine.1), channel_id=1, source_target_pairs={{0,128},{128,0},{1,129},{129,1},{2,130},{130,2},{3,131},{131,3},{4... | collective-permute-start | bytes 786440 | tf_op jit(solution)/shard_map/ppermute | solution.py:232
  2.3 0.7 convert_element_type.33
  3.0 1.0 fusion
  4.1 3.2 %constant_dynamic-slice_fusion = bf16[256,4096]{1,0:T(8,128)(2,1)} fusion(bf16[512,4096]{1,0:T(8,128)(2,1)} %w.1, s32[]{:T(128)S(6)} %select_n.3), kind=kLoop, calls=%fused_computation.6 | loop fusion | bytes 4194308 | tf_op jit(solution)/shard_map/dynamic_slice | solution.py:319
  7.3 3.0 %collective-permute-start.14 = (bf16[256,4096]{1,0:T(8,128)(2,1)}, bf16[256,4096]{1,0:T(8,128)(2,1)S(1)}, u32[]{:S(2)}, u32[]{:S(2)}) collective-permute-start(bf16[256,4096]{1,0:T(8,128)(2,1)} %constant_dynamic-slice_fusion), channel_id=1, source_target_pairs={{0,2},{2,0},{1,3},{3,1},{4,6},{6,4},{5,7},{7,5},{8,10},{10,8},{9,1... | collective-permute-start | bytes 6291464 | tf_op jit(solution)/shard_map/ppermute | solution.py:232
  10.4 2.0 %collective-permute-start.3 = (bf16[2,784,128]{2,1,0:T(8,128)(2,1)S(1)}, bf16[2,784,128]{2,1,0:T(8,128)(2,1)}, u32[]{:S(2)}, u32[]{:S(2)}) collective-permute-start(bf16[2,784,128]{2,1,0:T(8,128)(2,1)S(1)} %pad_maximum_fusion.refs_0_), channel_id=1, source_target_pairs={{0,16},{8,120},{16,32},{24,8},{32,48},{40,24},{48,64},{56,40},{64,... | collective-permute-start | bytes 1204232 | tf_op jit(solution)/shard_map/ppermute | solution.py:241
  12.4 4.5 %collective-permute-start.4 = (bf16[2,784,128]{2,1,0:T(8,128)(2,1)S(1)}, bf16[2,784,128]{2,1,0:T(8,128)(2,1)}, u32[]{:S(2)}, u32[]{:S(2)}) collective-permute-start(bf16[2,784,128]{2,1,0:T(8,128)(2,1)S(1)} %pad_maximum_fusion.refs_0_), channel_id=1, source_target_pairs={{0,32},{8,104},{16,48},{24,120},{32,64},{40,8},{48,80},{56,24},{64... | collective-permute-start | bytes 1204232 | tf_op jit(solution)/shard_map/ppermute | solution.py:241
  17.0 0.5 collective-permute-start.1
  17.5 5.3 %collective-permute-done.1.coarse_theirs = bf16[128,640]{1,0:T(8,128)(2,1)S(1)} collective-permute-done((bf16[128,640]{1,0:T(8,128)(2,1)S(1)}, bf16[128,640]{1,0:T(8,128)(2,1)S(1)}, u32[]{:S(2)}, u32[]{:S(2)}) %collective-permute-start.1) | collective-permute-done | bytes 163872 | tf_op jit(solution)/shard_map/ppermute | solution.py:232
  22.9 2.9 %fold.4 = (f32[4,512,128]{2,1,0:T(8,128)S(1)}, f32[4,512,256]{2,1,0:T(8,128)S(1)}, f32[4,256,128]{2,1,0:T(8,128)S(1)}, f32[4,256,256]{2,1,0:T(8,128)S(1)}) custom-call(bf16[512,512]{1,0:T(8,128)(2,1)S(1)} %get-tuple-element.33.q_ref, bf16[256,512]{1,0:T(8,128)(2,1)S(1)} %get-tuple-element.34.cq_ref, f32[256,128]{1,0:T(8,128)S(1)} %get-tuple-element.35.level_ref, ...), custom_call_target="tpu_custom_call" | custom-call | flops 1879048192 | bytes 262144 | tf_op jit(solution)/shard_map/fold/pallas_call | solution.py:146
  25.8 4.6 %collective-permute-done.4.refs_2_ = bf16[2,784,128]{2,1,0:T(8,128)(2,1)} collective-permute-done((bf16[2,784,128]{2,1,0:T(8,128)(2,1)S(1)}, bf16[2,784,128]{2,1,0:T(8,128)(2,1)}, u32[]{:S(2)}, u32[]{:S(2)}) %collective-permute-start.4) | collective-permute-done | bytes 401440 | tf_op jit(solution)/shard_map/ppermute | solution.py:241
  31.3 0.9 slice.27
  32.3 5.0 %collective-permute-start.8 = (bf16[1,784,128]{2,1,0:T(8,128)(2,1)S(1)}, bf16[1,784,128]{2,1,0:T(8,128)(2,1)S(1)}, u32[]{:S(2)}, u32[]{:S(2)}) collective-permute-start(bf16[1,784,128]{2,1,0:T(8,128)(2,1)S(1)} %slice.27), channel_id=1, source_target_pairs={{0,32},{8,104},{16,48},{24,120},{32,64},{40,8},{48,80},{56,24},{64... | collective-permute-start | bytes 602120 | tf_op jit(solution)/shard_map/ppermute | solution.py:241
  37.2 11.7 %fold.5 = (f32[4,512,128]{2,1,0:T(8,128)S(1)}, f32[4,512,256]{2,1,0:T(8,128)S(1)}, f32[4,256,128]{2,1,0:T(8,128)S(1)}, f32[4,256,256]{2,1,0:T(8,128)S(1)}) custom-call(bf16[512,512]{1,0:T(8,128)(2,1)S(1)} %get-tuple-element.33.q_ref, ...), custom_call_target="tpu_custom_call", output_to_operand_aliasing={{0}: (7, {}), {1}: (8, {}), {2}: (9, {}), {3}: (10, {})} | custom-call | flops 7516192768 | bytes 262144 | tf_op jit(solution)/shard_map/fold/pallas_call | solution.py:146
  49.6 1.5 %collective-permute-done.10.refs_3_ = bf16[1,784,128]{2,1,0:T(8,128)(2,1)S(1)} collective-permute-done((bf16[1,784,128]{2,1,0:T(8,128)(2,1)S(1)}, bf16[1,784,128]{2,1,0:T(8,128)(2,1)S(1)}, u32[]{:S(2)}, u32[]{:S(2)}) %collective-permute-start.10) | collective-permute-done | bytes 200736 | tf_op jit(solution)/shard_map/ppermute | solution.py:232
  51.1 4.5 %fold.7 = (bf16[192,640]{1,0:T(8,128)(2,1)S(1)}, bf16[192,640]{1,0:T(8,128)(2,1)S(1)}) custom-call(bf16[512,512]{1,0:T(8,128)(2,1)S(1)} %get-tuple-element.33.q_ref, bf16[256,512]{1,0:T(8,128)(2,1)S(1)} %get-tuple-element.34.cq_ref, f32[256,128]{1,0:T(8,128)S(1)} %get-tuple-element.35.level_ref, bf16[2,784,128]{2,1,0:T(8,128)(2,1)S(1)} %collective-permute-done.7.refs_0_, ...), custom_call_target="tpu_custom_call" | custom-call | flops 5505024 | bytes 262144 | tf_op jit(solution)/shard_map/fold/pallas_call | solution.py:146
  56.2 1.5 %collective-permute-start.13 = (bf16[192,640]{1,0:T(8,128)(2,1)S(1)}, bf16[192,640]{1,0:T(8,128)(2,1)S(1)}, u32[]{:S(2)}, u32[]{:S(2)}) collective-permute-start(bf16[192,640]{1,0:T(8,128)(2,1)S(1)} %get-tuple-element.59), channel_id=1, source_target_pairs={{0,130},{2,128},{128,2},{130,0},{1,131},{3,129},{129,3},{131,1},{4... | collective-permute-start | bytes 737288 | tf_op jit(solution)/shard_map/ppermute | solution.py:232
  57.7 4.5 %fold.6 = (bf16[192,640]{1,0:T(8,128)(2,1)S(1)}, bf16[192,640]{1,0:T(8,128)(2,1)S(1)}) custom-call(bf16[512,512]{1,0:T(8,128)(2,1)S(1)} %get-tuple-element.33.q_ref, bf16[256,512]{1,0:T(8,128)(2,1)S(1)} %get-tuple-element.34.cq_ref, f32[256,128]{1,0:T(8,128)S(1)} %get-tuple-element.35.level_ref, bf16[2,784,128]{2,1,0:T(8,128)(2,1)S(1)} %collective-permute-done.7.refs_0_, ...), custom_call_target="tpu_custom_call" | custom-call | flops 5505024 | bytes 262144 | tf_op jit(solution)/shard_map/fold/pallas_call | solution.py:146
  62.3 3.1 %collective-permute-start.12 = (bf16[192,640]{1,0:T(8,128)(2,1)S(1)}, bf16[192,640]{1,0:T(8,128)(2,1)S(1)}, u32[]{:S(2)}, u32[]{:S(2)}) collective-permute-start(bf16[192,640]{1,0:T(8,128)(2,1)S(1)} %get-tuple-element.58), channel_id=1, source_target_pairs={{0,2},{2,0},{1,3},{3,1},{4,6},{6,4},{5,7},{7,5},{8,10},{10,8},{9,1... | collective-permute-start | bytes 737288 | tf_op jit(solution)/shard_map/ppermute | solution.py:232
  65.4 3.6 %collective-permute-done.11.refs_1_.near = bf16[192,640]{1,0:T(8,128)(2,1)S(1)} collective-permute-done((bf16[192,640]{1,0:T(8,128)(2,1)S(1)}, bf16[192,640]{1,0:T(8,128)(2,1)S(1)}, u32[]{:S(2)}, u32[]{:S(2)}) %collective-permute-start.11) | collective-permute-done | bytes 245792 | tf_op jit(solution)/shard_map/ppermute | solution.py:232
  69.0 2.7 %collective-permute-done.12.refs_3_.cross = bf16[192,640]{1,0:T(8,128)(2,1)S(1)} collective-permute-done((bf16[192,640]{1,0:T(8,128)(2,1)S(1)}, bf16[192,640]{1,0:T(8,128)(2,1)S(1)}, u32[]{:S(2)}, u32[]{:S(2)}) %collective-permute-start.12) | collective-permute-done | bytes 245792 | tf_op jit(solution)/shard_map/ppermute | solution.py:232
  71.9 4.2 %collective-permute-done.15.w_other = bf16[256,4096]{1,0:T(8,128)(2,1)} collective-permute-done((bf16[256,4096]{1,0:T(8,128)(2,1)S(1)}, bf16[256,4096]{1,0:T(8,128)(2,1)}, u32[]{:S(2)}, u32[]{:S(2)}) %collective-permute-start.15) | collective-permute-done | bytes 2097184 | tf_op jit(solution)/shard_map/ppermute | solution.py:232
  76.1 2.2 %copy-done = bf16[512,4096]{1,0:T(8,128)(2,1)S(1)} copy-done((bf16[512,4096]{1,0:T(8,128)(2,1)S(1)}, bf16[512,4096]{1,0:T(8,128)(2,1)}, u32[]{:S(2)}) %copy-start) | copy-done | bytes 4194328
  78.2 5.5 %project.1 = (bf16[48,4096]{1,0:T(8,128)(2,1)S(1)}, bf16[48,4096]{1,0:T(8,128)(2,1)S(1)}, bf16[48,4096]{1,0:T(8,128)(2,1)S(1)}, bf16[48,4096]{1,0:T(8,128)(2,1)S(1)}) custom-call(s32[2]{0:T(128)S(1)} %pad_add_fusion.place_ref, bf16[192,640]{1,0:T(8,128)(2,1)S(1)} %get-tuple-element.56.keep, bf16[192,640]{1,0:T(8,128)(2,1)S(1)} %collective-permute-done.11.refs_1_.near, ...), custom_call_target="tpu_custom_call" | custom-call | flops 1610612736 | bytes 8388608 | tf_op jit(solution)/shard_map/project/pallas_call | solution.py:213
  83.8 1.1 %collective-permute-start.16 = (bf16[48,4096]{1,0:T(8,128)(2,1)S(1)}, bf16[48,4096]{1,0:T(8,128)(2,1)S(1)}, u32[]{:S(2)}, u32[]{:S(2)}) collective-permute-start(bf16[48,4096]{1,0:T(8,128)(2,1)S(1)} %get-tuple-element.61), channel_id=1, source_target_pairs={{0,1},{1,0},{2,3},{3,2},{4,5},{5,4},{6,7},{7,6},{8,9},{9,8},{10,11... | collective-permute-start | bytes 1179656 | tf_op jit(solution)/shard_map/ppermute | solution.py:232
  84.9 2.9 %collective-permute-start.17 = (bf16[48,4096]{1,0:T(8,128)(2,1)S(1)}, bf16[48,4096]{1,0:T(8,128)(2,1)S(1)}, u32[]{:S(2)}, u32[]{:S(2)}) collective-permute-start(bf16[48,4096]{1,0:T(8,128)(2,1)S(1)} %get-tuple-element.62), channel_id=1, source_target_pairs={{0,4},{4,0},{1,5},{5,1},{2,6},{6,2},{3,7},{7,3},{8,12},{12,8},{9,1... | collective-permute-start | bytes 1179656 | tf_op jit(solution)/shard_map/ppermute | solution.py:232
  87.8 1.0 collective-permute-start.18
  88.9 7.0 %collective-permute-done.16 = bf16[48,4096]{1,0:T(8,128)(2,1)S(1)} collective-permute-done((bf16[48,4096]{1,0:T(8,128)(2,1)S(1)}, bf16[48,4096]{1,0:T(8,128)(2,1)S(1)}, u32[]{:S(2)}, u32[]{:S(2)}) %collective-permute-start.16) | collective-permute-done | bytes 393248 | tf_op jit(solution)/shard_map/ppermute | solution.py:232
  95.8 8.8 %collective-permute-done.17 = bf16[48,4096]{1,0:T(8,128)(2,1)S(1)} collective-permute-done((bf16[48,4096]{1,0:T(8,128)(2,1)S(1)}, bf16[48,4096]{1,0:T(8,128)(2,1)S(1)}, u32[]{:S(2)}, u32[]{:S(2)}) %collective-permute-start.17) | collective-permute-done | bytes 393248 | tf_op jit(solution)/shard_map/ppermute | solution.py:232
  104.6 1.2 %collective-permute-done.18 = bf16[48,4096]{1,0:T(8,128)(2,1)S(1)} collective-permute-done((bf16[48,4096]{1,0:T(8,128)(2,1)S(1)}, bf16[48,4096]{1,0:T(8,128)(2,1)S(1)}, u32[]{:S(2)}, u32[]{:S(2)}) %collective-permute-start.18) | collective-permute-done | bytes 393248 | tf_op jit(solution)/shard_map/ppermute | solution.py:232
  105.8 0.7 add_convert_fusion.1
  106.5 0.8 add_convert_fusion
  (30 shorter events, 2.5 us)
Async XLA Ops:
  0.6 22.2 %collective-permute-start = (bf16[256,512]{1,0:T(8,128)(2,1)}, bf16[256,512]{1,0:T(8,128)(2,1)S(1)}, u32[]{:S(2)}, u32[]{:S(2)}) collective-permute-start(bf16[256,512]{1,0:T(8,128)(2,1)} %fine_mine.1), channel_id=1, source_target_pairs={{0,128},{128,0},{1,129},{129,1},{2,130},{130,2},{3,131},{131,3},{4... | collective-permute-start | bytes 786440 | tf_op jit(solution)/shard_map/ppermute | solution.py:232
  4.0 6.4 %collective-permute-start.2 = (bf16[784,128]{1,0:T(8,128)(2,1)S(1)}, bf16[784,128]{1,0:T(8,128)(2,1)S(1)}, u32[]{:S(2)}, u32[]{:S(2)}) collective-permute-start(bf16[784,128]{1,0:T(8,128)(2,1)S(1)} %get-tuple-element.65), channel_id=1, source_target_pairs={{0,8},{8,0},{1,9},{9,1},{2,10},{10,2},{3,11},{11,3},{4,12},{12,4},... | collective-permute-start | bytes 602120 | tf_op jit(solution)/shard_map/ppermute | solution.py:232
  4.1 12.9 %copy-start.2 = (bf16[128,512]{1,0:T(8,128)(2,1)S(1)}, bf16[128,512]{1,0:T(8,128)(2,1)}, u32[]{:S(2)}) copy-start(bf16[128,512]{1,0:T(8,128)(2,1)} %param.8) | copy-start | bytes 393220
  4.1 18.7 %copy-start.1 = (bf16[256,512]{1,0:T(8,128)(2,1)S(1)}, bf16[256,512]{1,0:T(8,128)(2,1)}, u32[]{:S(2)}) copy-start(bf16[256,512]{1,0:T(8,128)(2,1)} %fine_mine.1) | copy-start | bytes 786436
  7.3 64.5 %collective-permute-start.14 = (bf16[256,4096]{1,0:T(8,128)(2,1)}, bf16[256,4096]{1,0:T(8,128)(2,1)S(1)}, u32[]{:S(2)}, u32[]{:S(2)}) collective-permute-start(bf16[256,4096]{1,0:T(8,128)(2,1)} %constant_dynamic-slice_fusion), channel_id=1, source_target_pairs={{0,2},{2,0},{1,3},{3,1},{4,6},{6,4},{5,7},{7,5},{8,10},{10,8},{9,1... | collective-permute-start | bytes 6291464 | tf_op jit(solution)/shard_map/ppermute | solution.py:232
  10.4 15.5 %collective-permute-start.3 = (bf16[2,784,128]{2,1,0:T(8,128)(2,1)S(1)}, bf16[2,784,128]{2,1,0:T(8,128)(2,1)}, u32[]{:S(2)}, u32[]{:S(2)}) collective-permute-start(bf16[2,784,128]{2,1,0:T(8,128)(2,1)S(1)} %pad_maximum_fusion.refs_0_), channel_id=1, source_target_pairs={{0,16},{8,120},{16,32},{24,8},{32,48},{40,24},{48,64},{56,40},{64,... | collective-permute-start | bytes 1204232 | tf_op jit(solution)/shard_map/ppermute | solution.py:241
  12.4 18.0 %collective-permute-start.4 = (bf16[2,784,128]{2,1,0:T(8,128)(2,1)S(1)}, bf16[2,784,128]{2,1,0:T(8,128)(2,1)}, u32[]{:S(2)}, u32[]{:S(2)}) collective-permute-start(bf16[2,784,128]{2,1,0:T(8,128)(2,1)S(1)} %pad_maximum_fusion.refs_0_), channel_id=1, source_target_pairs={{0,32},{8,104},{16,48},{24,120},{32,64},{40,8},{48,80},{56,24},{64... | collective-permute-start | bytes 1204232 | tf_op jit(solution)/shard_map/ppermute | solution.py:241
  17.0 5.8 %collective-permute-start.1 = (bf16[128,640]{1,0:T(8,128)(2,1)S(1)}, bf16[128,640]{1,0:T(8,128)(2,1)S(1)}, u32[]{:S(2)}, u32[]{:S(2)}) collective-permute-start(bf16[128,640]{1,0:T(8,128)(2,1)S(1)} %pad_maximum_fusion.2.coarse_mine), channel_id=1, source_target_pairs={{0,128},{128,0},{1,129},{129,1},{2,130},{130,2},{3,131},{131,3},{4... | collective-permute-start | bytes 491528 | tf_op jit(solution)/shard_map/ppermute | solution.py:232
  30.4 6.8 %collective-permute-start.5 = (bf16[2,784,128]{2,1,0:T(8,128)(2,1)}, bf16[2,784,128]{2,1,0:T(8,128)(2,1)S(1)}, u32[]{:S(2)}, u32[]{:S(2)}) collective-permute-start(bf16[2,784,128]{2,1,0:T(8,128)(2,1)} %collective-permute-done.3.refs_0_), channel_id=1, source_target_pairs={{0,8},{8,0},{1,9},{9,1},{2,10},{10,2},{3,11},{11,3},{4,12},{12,4},... | collective-permute-start | bytes 1204232 | tf_op jit(solution)/shard_map/ppermute | solution.py:232
  30.4 6.8 %collective-permute-start.6 = (bf16[2,784,128]{2,1,0:T(8,128)(2,1)}, bf16[2,784,128]{2,1,0:T(8,128)(2,1)S(1)}, u32[]{:S(2)}, u32[]{:S(2)}) collective-permute-start(bf16[2,784,128]{2,1,0:T(8,128)(2,1)} %collective-permute-done.4.refs_2_), channel_id=1, source_target_pairs={{0,8},{8,0},{1,9},{9,1},{2,10},{10,2},{3,11},{11,3},{4,12},{12,4},... | collective-permute-start | bytes 1204232 | tf_op jit(solution)/shard_map/ppermute | solution.py:232
  30.9 18.1 %collective-permute-start.7 = (bf16[2,784,128]{2,1,0:T(8,128)(2,1)}, bf16[2,784,128]{2,1,0:T(8,128)(2,1)S(1)}, u32[]{:S(2)}, u32[]{:S(2)}) collective-permute-start(bf16[2,784,128]{2,1,0:T(8,128)(2,1)} %collective-permute-done.3.refs_0_), channel_id=1, source_target_pairs={{0,32},{8,104},{16,48},{24,120},{32,64},{40,8},{48,80},{56,24},{64... | collective-permute-start | bytes 1204232 | tf_op jit(solution)/shard_map/ppermute | solution.py:241
  32.3 16.7 %collective-permute-start.8 = (bf16[1,784,128]{2,1,0:T(8,128)(2,1)S(1)}, bf16[1,784,128]{2,1,0:T(8,128)(2,1)S(1)}, u32[]{:S(2)}, u32[]{:S(2)}) collective-permute-start(bf16[1,784,128]{2,1,0:T(8,128)(2,1)S(1)} %slice.27), channel_id=1, source_target_pairs={{0,32},{8,104},{16,48},{24,120},{32,64},{40,8},{48,80},{56,24},{64... | collective-permute-start | bytes 602120 | tf_op jit(solution)/shard_map/ppermute | solution.py:241
  49.0 2.1 %collective-permute-start.9 = (bf16[2,784,128]{2,1,0:T(8,128)(2,1)S(1)}, bf16[2,784,128]{2,1,0:T(8,128)(2,1)S(1)}, u32[]{:S(2)}, u32[]{:S(2)}) collective-permute-start(bf16[2,784,128]{2,1,0:T(8,128)(2,1)S(1)} %collective-permute-done.7.refs_0_), channel_id=1, source_target_pairs={{0,8},{8,0},{1,9},{9,1},{2,10},{10,2},{3,11},{11,3},{4,12},{12,4},... | collective-permute-start | bytes 1204232 | tf_op jit(solution)/shard_map/ppermute | solution.py:232
  49.1 2.0 %collective-permute-start.10 = (bf16[1,784,128]{2,1,0:T(8,128)(2,1)S(1)}, bf16[1,784,128]{2,1,0:T(8,128)(2,1)S(1)}, u32[]{:S(2)}, u32[]{:S(2)}) collective-permute-start(bf16[1,784,128]{2,1,0:T(8,128)(2,1)S(1)} %collective-permute-done.8.refs_2_), channel_id=1, source_target_pairs={{0,8},{8,0},{1,9},{9,1},{2,10},{10,2},{3,11},{11,3},{4,12},{12,4},... | collective-permute-start | bytes 602120 | tf_op jit(solution)/shard_map/ppermute | solution.py:232
  55.7 13.4 %collective-permute-start.11 = (bf16[192,640]{1,0:T(8,128)(2,1)S(1)}, bf16[192,640]{1,0:T(8,128)(2,1)S(1)}, u32[]{:S(2)}, u32[]{:S(2)}) collective-permute-start(bf16[192,640]{1,0:T(8,128)(2,1)S(1)} %get-tuple-element.57), channel_id=1, source_target_pairs={{0,128},{128,0},{1,129},{129,1},{2,130},{130,2},{3,131},{131,3},{4... | collective-permute-start | bytes 737288 | tf_op jit(solution)/shard_map/ppermute | solution.py:232
  56.2 12.8 %collective-permute-start.13 = (bf16[192,640]{1,0:T(8,128)(2,1)S(1)}, bf16[192,640]{1,0:T(8,128)(2,1)S(1)}, u32[]{:S(2)}, u32[]{:S(2)}) collective-permute-start(bf16[192,640]{1,0:T(8,128)(2,1)S(1)} %get-tuple-element.59), channel_id=1, source_target_pairs={{0,130},{2,128},{128,2},{130,0},{1,131},{3,129},{129,3},{131,1},{4... | collective-permute-start | bytes 737288 | tf_op jit(solution)/shard_map/ppermute | solution.py:232
  62.3 9.5 %collective-permute-start.12 = (bf16[192,640]{1,0:T(8,128)(2,1)S(1)}, bf16[192,640]{1,0:T(8,128)(2,1)S(1)}, u32[]{:S(2)}, u32[]{:S(2)}) collective-permute-start(bf16[192,640]{1,0:T(8,128)(2,1)S(1)} %get-tuple-element.58), channel_id=1, source_target_pairs={{0,2},{2,0},{1,3},{3,1},{4,6},{6,4},{5,7},{7,5},{8,10},{10,8},{9,1... | collective-permute-start | bytes 737288 | tf_op jit(solution)/shard_map/ppermute | solution.py:232
  71.8 4.3 %collective-permute-start.15 = (bf16[256,4096]{1,0:T(8,128)(2,1)S(1)}, bf16[256,4096]{1,0:T(8,128)(2,1)}, u32[]{:S(2)}, u32[]{:S(2)}) collective-permute-start(bf16[256,4096]{1,0:T(8,128)(2,1)S(1)} %after.1.w_mine), channel_id=1, source_target_pairs={{0,8},{8,0},{1,9},{9,1},{2,10},{10,2},{3,11},{11,3},{4,12},{12,4},... | collective-permute-start | bytes 6291464 | tf_op jit(solution)/shard_map/ppermute | solution.py:232
  76.1 2.2 %copy-start = (bf16[512,4096]{1,0:T(8,128)(2,1)S(1)}, bf16[512,4096]{1,0:T(8,128)(2,1)}, u32[]{:S(2)}) copy-start(bf16[512,4096]{1,0:T(8,128)(2,1)} %w.1) | copy-start | bytes 12582916
  83.8 12.0 %collective-permute-start.16 = (bf16[48,4096]{1,0:T(8,128)(2,1)S(1)}, bf16[48,4096]{1,0:T(8,128)(2,1)S(1)}, u32[]{:S(2)}, u32[]{:S(2)}) collective-permute-start(bf16[48,4096]{1,0:T(8,128)(2,1)S(1)} %get-tuple-element.61), channel_id=1, source_target_pairs={{0,1},{1,0},{2,3},{3,2},{4,5},{5,4},{6,7},{7,6},{8,9},{9,8},{10,11... | collective-permute-start | bytes 1179656 | tf_op jit(solution)/shard_map/ppermute | solution.py:232
  84.9 19.7 %collective-permute-start.17 = (bf16[48,4096]{1,0:T(8,128)(2,1)S(1)}, bf16[48,4096]{1,0:T(8,128)(2,1)S(1)}, u32[]{:S(2)}, u32[]{:S(2)}) collective-permute-start(bf16[48,4096]{1,0:T(8,128)(2,1)S(1)} %get-tuple-element.62), channel_id=1, source_target_pairs={{0,4},{4,0},{1,5},{5,1},{2,6},{6,2},{3,7},{7,3},{8,12},{12,8},{9,1... | collective-permute-start | bytes 1179656 | tf_op jit(solution)/shard_map/ppermute | solution.py:232
  87.8 18.0 %collective-permute-start.18 = (bf16[48,4096]{1,0:T(8,128)(2,1)S(1)}, bf16[48,4096]{1,0:T(8,128)(2,1)S(1)}, u32[]{:S(2)}, u32[]{:S(2)}) collective-permute-start(bf16[48,4096]{1,0:T(8,128)(2,1)S(1)} %get-tuple-element.63), channel_id=1, source_target_pairs={{0,5},{1,4},{4,1},{5,0},{2,7},{3,6},{6,3},{7,2},{8,13},{9,12},{12,... | collective-permute-start | bytes 1179656 | tf_op jit(solution)/shard_map/ppermute | solution.py:232

commit v4 on v3

--- a/solution.py
+++ b/solution.py
@@ -157,8 +157,7 @@
     )(*ins)
 
 
-def project_kernel(n_fine, n_blocks, place_ref, keep, near, cross, far, w, w_mine, w_other, *refs):
-    outs, a_ref = refs[:-1], refs[-1]
+def project_kernel(n_fine, n_blocks, place_ref, keep, near, cross, far, w, w_mine, share_ref, rest_ref, a_ref):
     heads = keep.shape[1] // HD - 1
     rows = keep.shape[0]
     width = heads * HD
@@ -195,36 +194,65 @@
                     n_fine + b * c : n_fine + (b + 1) * c
                 ]
 
-    share = (
-        dot_nn(a_ref[:, :width], w[...])
-        + dot_nn(a_ref[:, width : width + half], w_mine[...])
-        + dot_nn(a_ref[:, width + half :], w_other[...])
-    ).astype(jnp.bfloat16)
-    size = rows // n_blocks
-    for i, out in enumerate(outs):
-        out[...] = share[i * size : (i + 1) * size]
+        rest_ref[...] = a_ref[:, width + half :]
+
+    share_ref[...] = dot_nn(a_ref[:, :width], w[...]) + dot_nn(
+        a_ref[:, width : width + half], w_mine[...]
+    )
 
 
 def project(places, parts, weights, n_fine, n_blocks):
     rows = parts[0].shape[0]
     columns = weights[0].shape[1]
     tile = math.gcd(columns, 1024)
-    depth = sum(w.shape[0] for w in weights)
+    half = weights[1].shape[0]
+    depth = weights[0].shape[0] + 2 * half
     return pl.pallas_call(
         functools.partial(project_kernel, n_fine, n_blocks),
         grid=(columns // tile,),
-        out_shape=(jax.ShapeDtypeStruct((rows // n_blocks, columns), jnp.bfloat16),) * n_blocks,
+        out_shape=(
+            jax.ShapeDtypeStruct((rows, columns), jnp.float32),
+            jax.ShapeDtypeStruct((rows, half), jnp.bfloat16),
+        ),
         in_specs=[pl.BlockSpec(memory_space=pltpu.SMEM)]
         + [whole(p.shape) for p in parts]
         + [pl.BlockSpec((w.shape[0], tile), lambda j: (0, j)) for w in weights],
-        out_specs=(pl.BlockSpec((rows // n_blocks, tile), lambda j: (0, j)),) * n_blocks,
+        out_specs=(pl.BlockSpec((rows, tile), lambda j: (0, j)), whole((rows, half))),
         scratch_shapes=[pltpu.VMEM((rows, depth), jnp.bfloat16)],
         compiler_params=pltpu.CompilerParams(vmem_limit_bytes=GRANT),
         cost_estimate=pl.CostEstimate(
-            flops=2 * rows * depth * columns, bytes_accessed=2 * depth * columns, transcendentals=0
+            flops=2 * rows * (depth - half) * columns, bytes_accessed=2 * depth * columns, transcendentals=0
         ),
         name="project",
     )(places, *parts, *weights)
+
+
+def complete_kernel(share_ref, rest_ref, w, *outs):
+    share = (share_ref[...] + dot_nn(rest_ref[...], w[...])).astype(jnp.bfloat16)
+    size = share.shape[0] // len(outs)
+    for i, out in enumerate(outs):
+        out[...] = share[i * size : (i + 1) * size]
+
+
+def completed(share, rest, weight, n_blocks):
+    rows, columns = share.shape
+    tile = math.gcd(columns, 1024)
+    return pl.pallas_call(
+        complete_kernel,
+        grid=(columns // tile,),
+        out_shape=(jax.ShapeDtypeStruct((rows // n_blocks, columns), jnp.bfloat16),) * n_blocks,
+        in_specs=[
+            pl.BlockSpec((rows, tile), lambda j: (0, j)),
+            whole(rest.shape),
+            pl.BlockSpec((weight.shape[0], tile), lambda j: (0, j)),
+        ],
+        out_specs=(pl.BlockSpec((rows // n_blocks, tile), lambda j: (0, j)),) * n_blocks,
+        compiler_params=pltpu.CompilerParams(vmem_limit_bytes=GRANT),
+        cost_estimate=pl.CostEstimate(
+            flops=2 * rows * weight.size, bytes_accessed=4 * share.size, transcendentals=0
+        ),
+        name="complete",
+    )(share, rest, weight)
 
 
 def crossed(x, axes):
@@ -340,13 +368,14 @@
     across = crossed(to_xp, ("xp",))
     weight_mine = after(weight_mine, (near, far, across))
     weight_other = crossed(weight_mine, ("c",))
-    shares = project(
+    share, rest = project(
         jnp.stack([core, lax.axis_index((HEAD[0], HEAD[2]))]),
         (keep, near, across, far),
-        (out_weight, weight_mine, weight_other),
+        (out_weight, weight_mine),
         fine // 2,
         4,
     )
+    shares = completed(share, rest, weight_other, 4)
     got = [shares[0]]
     for share, axes in zip(shares[1:], ((HEAD[2],), (HEAD[0],), (HEAD[0], HEAD[2]))):
         got.append(crossed(share, axes))

time: 108 us -> 106 us (0.981)
  waiting for transfers between devices: 38.9 us -> 35 us
  Pallas kernels: 29.4 us -> 31.3 us
    ppermute x15, waiting for transfers between devices: 34.3 us -> 30.5 us  [crossed(): return lax.ppermute(x, axes, [(i, n - 1 - i) for i in range(n)])]
    pallas_call x0 -> x1, Pallas kernels: none -> 3.21 us  [completed(): pl.pallas_call(complete_kernel, grid=(columns // tile,), out_shape=(jax.S...]
    pallas_call x1, Pallas kernels: 5.52 us -> 4.21 us  [project(): pl.pallas_call(functools.partial(project_kernel, n_fine, n_blocks), grid=...]
  transfers between devices with their start and end apart: 19 -> 19, of which waited for: 9 -> 8; matrix products, arithmetic and copies ran while one was open for 6% -> 6% of each run, Pallas kernels for 22% -> 27%
where the time goes in v4:
time: 106 us; the launch traced here: 105 us
  waiting for transfers between devices  35 us (33%)
  Pallas kernels  31.3 us (30%)
  starting transfers between devices  28.5 us (27%)
  local copies, waits for them, and re-layouts  6.43 us (6%)
  other arithmetic  3.34 us (3%)
    ppermute x15, waiting for transfers between devices, crossed(): return lax.ppermute(x, axes, [(i, n - 1 - i) for i in range(n)])  30.5 us
    pallas_call x4, Pallas kernels, fold(): pl.pallas_call(functools.partial(fold_kernel, len(blocks), fine, coarse,...  23.8 us
    ppermute x15, starting transfers between devices, crossed(): return lax.ppermute(x, axes, [(i, n - 1 - i) for i in range(n)])  16.7 us
    ppermute x4, starting transfers between devices, along_z(): return lax.ppermute(x, ('z', 'c'), pairs)  11.9 us
    ppermute x4, waiting for transfers between devices, along_z(): return lax.ppermute(x, ('z', 'c'), pairs)  4.57 us
    pallas_call x1, Pallas kernels, project(): pl.pallas_call(functools.partial(project_kernel, n_fine, n_blocks), grid=...  4.21 us
    pallas_call x1, Pallas kernels, completed(): pl.pallas_call(complete_kernel, grid=(columns // tile,), out_shape=(jax.S...  3.21 us
    dynamic_slice x1, local copies, waits for them, and re-layouts, per_device(): lax.dynamic_slice_in_dim(out_weight, core * depth, depth, 0)  3.2 us
  transfers between devices with their start and end apart: 19, of which 8 were waited for; matrix products, arithmetic and copies ran while one was open for 6% of the time, Pallas kernels for 27%

profile of v4, /device:TPU:32, one launch (start us, length us, event | category | flops | bytes accessed | tf_op | source)
XLA Modules:
  0.0 105.4 jit_solution(459101338196140739)
XLA Ops:
  0.6 1.7 %collective-permute-start = (bf16[256,512]{1,0:T(8,128)(2,1)}, bf16[256,512]{1,0:T(8,128)(2,1)S(1)}, u32[]{:S(2)}, u32[]{:S(2)}) collective-permute-start(bf16[256,512]{1,0:T(8,128)(2,1)} %fine_mine.1), channel_id=1, source_target_pairs={{0,128},{128,0},{1,129},{129,1},{2,130},{130,2},{3,131},{131,3},{4... | collective-permute-start | bytes 786440 | tf_op jit(solution)/shard_map/ppermute | solution.py:260
  2.3 0.7 convert_element_type.33
  3.0 1.0 fusion
  4.1 3.2 %constant_dynamic-slice_fusion = bf16[256,4096]{1,0:T(8,128)(2,1)} fusion(bf16[512,4096]{1,0:T(8,128)(2,1)} %w.1, s32[]{:T(128)S(6)} %select_n.3), kind=kLoop, calls=%fused_computation.6 | loop fusion | bytes 4194308 | tf_op jit(solution)/shard_map/dynamic_slice | solution.py:347
  7.3 3.0 %collective-permute-start.14 = (bf16[256,4096]{1,0:T(8,128)(2,1)}, bf16[256,4096]{1,0:T(8,128)(2,1)S(1)}, u32[]{:S(2)}, u32[]{:S(2)}) collective-permute-start(bf16[256,4096]{1,0:T(8,128)(2,1)} %constant_dynamic-slice_fusion), channel_id=1, source_target_pairs={{0,2},{2,0},{1,3},{3,1},{4,6},{6,4},{5,7},{7,5},{8,10},{10,8},{9,1... | collective-permute-start | bytes 6291464 | tf_op jit(solution)/shard_map/ppermute | solution.py:260
  10.4 2.0 %collective-permute-start.3 = (bf16[2,784,128]{2,1,0:T(8,128)(2,1)S(1)}, bf16[2,784,128]{2,1,0:T(8,128)(2,1)}, u32[]{:S(2)}, u32[]{:S(2)}) collective-permute-start(bf16[2,784,128]{2,1,0:T(8,128)(2,1)S(1)} %pad_maximum_fusion.refs_0_), channel_id=1, source_target_pairs={{0,16},{8,120},{16,32},{24,8},{32,48},{40,24},{48,64},{56,40},{64,... | collective-permute-start | bytes 1204232 | tf_op jit(solution)/shard_map/ppermute | solution.py:269
  12.4 4.5 %collective-permute-start.4 = (bf16[2,784,128]{2,1,0:T(8,128)(2,1)S(1)}, bf16[2,784,128]{2,1,0:T(8,128)(2,1)}, u32[]{:S(2)}, u32[]{:S(2)}) collective-permute-start(bf16[2,784,128]{2,1,0:T(8,128)(2,1)S(1)} %pad_maximum_fusion.refs_0_), channel_id=1, source_target_pairs={{0,32},{8,104},{16,48},{24,120},{32,64},{40,8},{48,80},{56,24},{64... | collective-permute-start | bytes 1204232 | tf_op jit(solution)/shard_map/ppermute | solution.py:269
  17.5 5.3 %collective-permute-done.1.coarse_theirs = bf16[128,640]{1,0:T(8,128)(2,1)S(1)} collective-permute-done((bf16[128,640]{1,0:T(8,128)(2,1)S(1)}, bf16[128,640]{1,0:T(8,128)(2,1)S(1)}, u32[]{:S(2)}, u32[]{:S(2)}) %collective-permute-start.1) | collective-permute-done | bytes 163872 | tf_op jit(solution)/shard_map/ppermute | solution.py:260
  22.9 2.9 %fold.4 = (f32[4,512,128]{2,1,0:T(8,128)S(1)}, f32[4,512,256]{2,1,0:T(8,128)S(1)}, f32[4,256,128]{2,1,0:T(8,128)S(1)}, f32[4,256,256]{2,1,0:T(8,128)S(1)}) custom-call(bf16[512,512]{1,0:T(8,128)(2,1)S(1)} %get-tuple-element.35.q_ref, bf16[256,512]{1,0:T(8,128)(2,1)S(1)} %get-tuple-element.36.cq_ref, f32[256,128]{1,0:T(8,128)S(1)} %get-tuple-element.37.level_ref, ...), custom_call_target="tpu_custom_call" | custom-call | flops 1879048192 | bytes 262144 | tf_op jit(solution)/shard_map/fold/pallas_call | solution.py:146
  25.8 4.6 %collective-permute-done.4.refs_2_ = bf16[2,784,128]{2,1,0:T(8,128)(2,1)} collective-permute-done((bf16[2,784,128]{2,1,0:T(8,128)(2,1)S(1)}, bf16[2,784,128]{2,1,0:T(8,128)(2,1)}, u32[]{:S(2)}, u32[]{:S(2)}) %collective-permute-start.4) | collective-permute-done | bytes 401440 | tf_op jit(solution)/shard_map/ppermute | solution.py:269
  31.3 0.9 slice.27
  32.3 5.0 %collective-permute-start.8 = (bf16[1,784,128]{2,1,0:T(8,128)(2,1)S(1)}, bf16[1,784,128]{2,1,0:T(8,128)(2,1)S(1)}, u32[]{:S(2)}, u32[]{:S(2)}) collective-permute-start(bf16[1,784,128]{2,1,0:T(8,128)(2,1)S(1)} %slice.27), channel_id=1, source_target_pairs={{0,32},{8,104},{16,48},{24,120},{32,64},{40,8},{48,80},{56,24},{64... | collective-permute-start | bytes 602120 | tf_op jit(solution)/shard_map/ppermute | solution.py:269
  37.2 11.7 %fold.5 = (f32[4,512,128]{2,1,0:T(8,128)S(1)}, f32[4,512,256]{2,1,0:T(8,128)S(1)}, f32[4,256,128]{2,1,0:T(8,128)S(1)}, f32[4,256,256]{2,1,0:T(8,128)S(1)}) custom-call(bf16[512,512]{1,0:T(8,128)(2,1)S(1)} %get-tuple-element.35.q_ref, ...), custom_call_target="tpu_custom_call", output_to_operand_aliasing={{0}: (7, {}), {1}: (8, {}), {2}: (9, {}), {3}: (10, {})} | custom-call | flops 7516192768 | bytes 262144 | tf_op jit(solution)/shard_map/fold/pallas_call | solution.py:146
  49.6 1.5 %collective-permute-done.10.refs_3_ = bf16[1,784,128]{2,1,0:T(8,128)(2,1)S(1)} collective-permute-done((bf16[1,784,128]{2,1,0:T(8,128)(2,1)S(1)}, bf16[1,784,128]{2,1,0:T(8,128)(2,1)S(1)}, u32[]{:S(2)}, u32[]{:S(2)}) %collective-permute-start.10) | collective-permute-done | bytes 200736 | tf_op jit(solution)/shard_map/ppermute | solution.py:260
  51.1 4.5 %fold.7 = (bf16[192,640]{1,0:T(8,128)(2,1)S(1)}, bf16[192,640]{1,0:T(8,128)(2,1)S(1)}) custom-call(bf16[512,512]{1,0:T(8,128)(2,1)S(1)} %get-tuple-element.35.q_ref, bf16[256,512]{1,0:T(8,128)(2,1)S(1)} %get-tuple-element.36.cq_ref, f32[256,128]{1,0:T(8,128)S(1)} %get-tuple-element.37.level_ref, bf16[2,784,128]{2,1,0:T(8,128)(2,1)S(1)} %collective-permute-done.7.refs_0_, ...), custom_call_target="tpu_custom_call" | custom-call | flops 5505024 | bytes 262144 | tf_op jit(solution)/shard_map/fold/pallas_call | solution.py:146
  55.7 0.5 collective-permute-start.11
  56.2 1.5 %collective-permute-start.13 = (bf16[192,640]{1,0:T(8,128)(2,1)S(1)}, bf16[192,640]{1,0:T(8,128)(2,1)S(1)}, u32[]{:S(2)}, u32[]{:S(2)}) collective-permute-start(bf16[192,640]{1,0:T(8,128)(2,1)S(1)} %get-tuple-element.61), channel_id=1, source_target_pairs={{0,130},{2,128},{128,2},{130,0},{1,131},{3,129},{129,3},{131,1},{4... | collective-permute-start | bytes 737288 | tf_op jit(solution)/shard_map/ppermute | solution.py:260
  57.7 4.5 %fold.6 = (bf16[192,640]{1,0:T(8,128)(2,1)S(1)}, bf16[192,640]{1,0:T(8,128)(2,1)S(1)}) custom-call(bf16[512,512]{1,0:T(8,128)(2,1)S(1)} %get-tuple-element.35.q_ref, bf16[256,512]{1,0:T(8,128)(2,1)S(1)} %get-tuple-element.36.cq_ref, f32[256,128]{1,0:T(8,128)S(1)} %get-tuple-element.37.level_ref, bf16[2,784,128]{2,1,0:T(8,128)(2,1)S(1)} %collective-permute-done.7.refs_0_, ...), custom_call_target="tpu_custom_call" | custom-call | flops 5505024 | bytes 262144 | tf_op jit(solution)/shard_map/fold/pallas_call | solution.py:146
  62.3 3.1 %collective-permute-start.12 = (bf16[192,640]{1,0:T(8,128)(2,1)S(1)}, bf16[192,640]{1,0:T(8,128)(2,1)S(1)}, u32[]{:S(2)}, u32[]{:S(2)}) collective-permute-start(bf16[192,640]{1,0:T(8,128)(2,1)S(1)} %get-tuple-element.60), channel_id=1, source_target_pairs={{0,2},{2,0},{1,3},{3,1},{4,6},{6,4},{5,7},{7,5},{8,10},{10,8},{9,1... | collective-permute-start | bytes 737288 | tf_op jit(solution)/shard_map/ppermute | solution.py:260
  65.4 3.6 %collective-permute-done.11.refs_1_.near = bf16[192,640]{1,0:T(8,128)(2,1)S(1)} collective-permute-done((bf16[192,640]{1,0:T(8,128)(2,1)S(1)}, bf16[192,640]{1,0:T(8,128)(2,1)S(1)}, u32[]{:S(2)}, u32[]{:S(2)}) %collective-permute-start.11) | collective-permute-done | bytes 245792 | tf_op jit(solution)/shard_map/ppermute | solution.py:260
  69.0 2.7 %collective-permute-done.12.refs_3_.cross = bf16[192,640]{1,0:T(8,128)(2,1)S(1)} collective-permute-done((bf16[192,640]{1,0:T(8,128)(2,1)S(1)}, bf16[192,640]{1,0:T(8,128)(2,1)S(1)}, u32[]{:S(2)}, u32[]{:S(2)}) %collective-permute-start.12) | collective-permute-done | bytes 245792 | tf_op jit(solution)/shard_map/ppermute | solution.py:260
  71.8 2.2 %copy-done = bf16[512,4096]{1,0:T(8,128)(2,1)S(1)} copy-done((bf16[512,4096]{1,0:T(8,128)(2,1)S(1)}, bf16[512,4096]{1,0:T(8,128)(2,1)}, u32[]{:S(2)}) %copy-start) | copy-done | bytes 4194328
  74.0 4.2 %project.1 = (f32[192,4096]{1,0:T(8,128)S(1)}, bf16[192,256]{1,0:T(8,128)(2,1)S(1)}) custom-call(s32[2]{0:T(128)S(1)} %pad_add_fusion.place_ref, bf16[192,640]{1,0:T(8,128)(2,1)S(1)} %get-tuple-element.58.keep, bf16[192,640]{1,0:T(8,128)(2,1)S(1)} %collective-permute-done.11.refs_1_.near, bf16[192,640]{1,0:T(8,128)(2,1)S(1)} %collective-permute-done.12.refs_3_.cross, ...), custom_call_target="tpu_custom_call" | custom-call | flops 1207959552 | bytes 8388608 | tf_op jit(solution)/shard_map/project/pallas_call | solution.py:210
  78.3 3.2 %complete.1 = (bf16[48,4096]{1,0:T(8,128)(2,1)S(1)}, bf16[48,4096]{1,0:T(8,128)(2,1)S(1)}, bf16[48,4096]{1,0:T(8,128)(2,1)S(1)}, bf16[48,4096]{1,0:T(8,128)(2,1)S(1)}) custom-call(f32[192,4096]{1,0:T(8,128)S(1)} %get-tuple-element.62.share_ref, bf16[192,256]{1,0:T(8,128)(2,1)S(1)} %get-tuple-element.63.rest_ref, bf16[256,4096]{1,0:T(8,128)(2,1)} %collective-permute-done.15.w), custom_call_target="tpu_custom_call" | custom-call | flops 402653184 | bytes 3145728 | tf_op jit(solution)/shard_map/complete/pallas_call | solution.py:240
  81.5 1.1 %collective-permute-start.16 = (bf16[48,4096]{1,0:T(8,128)(2,1)S(1)}, bf16[48,4096]{1,0:T(8,128)(2,1)S(1)}, u32[]{:S(2)}, u32[]{:S(2)}) collective-permute-start(bf16[48,4096]{1,0:T(8,128)(2,1)S(1)} %get-tuple-element.65), channel_id=1, source_target_pairs={{0,1},{1,0},{2,3},{3,2},{4,5},{5,4},{6,7},{7,6},{8,9},{9,8},{10,11... | collective-permute-start | bytes 1179656 | tf_op jit(solution)/shard_map/ppermute | solution.py:260
  82.6 2.9 %collective-permute-start.17 = (bf16[48,4096]{1,0:T(8,128)(2,1)S(1)}, bf16[48,4096]{1,0:T(8,128)(2,1)S(1)}, u32[]{:S(2)}, u32[]{:S(2)}) collective-permute-start(bf16[48,4096]{1,0:T(8,128)(2,1)S(1)} %get-tuple-element.66), channel_id=1, source_target_pairs={{0,4},{4,0},{1,5},{5,1},{2,6},{6,2},{3,7},{7,3},{8,12},{12,8},{9,1... | collective-permute-start | bytes 1179656 | tf_op jit(solution)/shard_map/ppermute | solution.py:260
  85.5 1.0 collective-permute-start.18
  86.6 6.9 %collective-permute-done.16 = bf16[48,4096]{1,0:T(8,128)(2,1)S(1)} collective-permute-done((bf16[48,4096]{1,0:T(8,128)(2,1)S(1)}, bf16[48,4096]{1,0:T(8,128)(2,1)S(1)}, u32[]{:S(2)}, u32[]{:S(2)}) %collective-permute-start.16) | collective-permute-done | bytes 393248 | tf_op jit(solution)/shard_map/ppermute | solution.py:260
  93.5 9.2 %collective-permute-done.17 = bf16[48,4096]{1,0:T(8,128)(2,1)S(1)} collective-permute-done((bf16[48,4096]{1,0:T(8,128)(2,1)S(1)}, bf16[48,4096]{1,0:T(8,128)(2,1)S(1)}, u32[]{:S(2)}, u32[]{:S(2)}) %collective-permute-start.17) | collective-permute-done | bytes 393248 | tf_op jit(solution)/shard_map/ppermute | solution.py:260
  102.7 1.1 %collective-permute-done.18 = bf16[48,4096]{1,0:T(8,128)(2,1)S(1)} collective-permute-done((bf16[48,4096]{1,0:T(8,128)(2,1)S(1)}, bf16[48,4096]{1,0:T(8,128)(2,1)S(1)}, u32[]{:S(2)}, u32[]{:S(2)}) %collective-permute-start.18) | collective-permute-done | bytes 393248 | tf_op jit(solution)/shard_map/ppermute | solution.py:260
  103.8 0.7 add_convert_fusion.1
  104.6 0.8 add_convert_fusion
  (31 shorter events, 2.5 us)
Async XLA Ops:
  0.6 22.2 %collective-permute-start = (bf16[256,512]{1,0:T(8,128)(2,1)}, bf16[256,512]{1,0:T(8,128)(2,1)S(1)}, u32[]{:S(2)}, u32[]{:S(2)}) collective-permute-start(bf16[256,512]{1,0:T(8,128)(2,1)} %fine_mine.1), channel_id=1, source_target_pairs={{0,128},{128,0},{1,129},{129,1},{2,130},{130,2},{3,131},{131,3},{4... | collective-permute-start | bytes 786440 | tf_op jit(solution)/shard_map/ppermute | solution.py:260
  4.0 6.4 %collective-permute-start.2 = (bf16[784,128]{1,0:T(8,128)(2,1)S(1)}, bf16[784,128]{1,0:T(8,128)(2,1)S(1)}, u32[]{:S(2)}, u32[]{:S(2)}) collective-permute-start(bf16[784,128]{1,0:T(8,128)(2,1)S(1)} %get-tuple-element.69), channel_id=1, source_target_pairs={{0,8},{8,0},{1,9},{9,1},{2,10},{10,2},{3,11},{11,3},{4,12},{12,4},... | collective-permute-start | bytes 602120 | tf_op jit(solution)/shard_map/ppermute | solution.py:260
  4.1 12.9 %copy-start.2 = (bf16[128,512]{1,0:T(8,128)(2,1)S(1)}, bf16[128,512]{1,0:T(8,128)(2,1)}, u32[]{:S(2)}) copy-start(bf16[128,512]{1,0:T(8,128)(2,1)} %param.8) | copy-start | bytes 393220
  4.1 18.7 %copy-start.1 = (bf16[256,512]{1,0:T(8,128)(2,1)S(1)}, bf16[256,512]{1,0:T(8,128)(2,1)}, u32[]{:S(2)}) copy-start(bf16[256,512]{1,0:T(8,128)(2,1)} %fine_mine.1) | copy-start | bytes 786436
  7.3 64.5 %collective-permute-start.14 = (bf16[256,4096]{1,0:T(8,128)(2,1)}, bf16[256,4096]{1,0:T(8,128)(2,1)S(1)}, u32[]{:S(2)}, u32[]{:S(2)}) collective-permute-start(bf16[256,4096]{1,0:T(8,128)(2,1)} %constant_dynamic-slice_fusion), channel_id=1, source_target_pairs={{0,2},{2,0},{1,3},{3,1},{4,6},{6,4},{5,7},{7,5},{8,10},{10,8},{9,1... | collective-permute-start | bytes 6291464 | tf_op jit(solution)/shard_map/ppermute | solution.py:260
  10.4 15.5 %collective-permute-start.3 = (bf16[2,784,128]{2,1,0:T(8,128)(2,1)S(1)}, bf16[2,784,128]{2,1,0:T(8,128)(2,1)}, u32[]{:S(2)}, u32[]{:S(2)}) collective-permute-start(bf16[2,784,128]{2,1,0:T(8,128)(2,1)S(1)} %pad_maximum_fusion.refs_0_), channel_id=1, source_target_pairs={{0,16},{8,120},{16,32},{24,8},{32,48},{40,24},{48,64},{56,40},{64,... | collective-permute-start | bytes 1204232 | tf_op jit(solution)/shard_map/ppermute | solution.py:269
  12.4 18.0 %collective-permute-start.4 = (bf16[2,784,128]{2,1,0:T(8,128)(2,1)S(1)}, bf16[2,784,128]{2,1,0:T(8,128)(2,1)}, u32[]{:S(2)}, u32[]{:S(2)}) collective-permute-start(bf16[2,784,128]{2,1,0:T(8,128)(2,1)S(1)} %pad_maximum_fusion.refs_0_), channel_id=1, source_target_pairs={{0,32},{8,104},{16,48},{24,120},{32,64},{40,8},{48,80},{56,24},{64... | collective-permute-start | bytes 1204232 | tf_op jit(solution)/shard_map/ppermute | solution.py:269
  17.0 5.8 %collective-permute-start.1 = (bf16[128,640]{1,0:T(8,128)(2,1)S(1)}, bf16[128,640]{1,0:T(8,128)(2,1)S(1)}, u32[]{:S(2)}, u32[]{:S(2)}) collective-permute-start(bf16[128,640]{1,0:T(8,128)(2,1)S(1)} %pad_maximum_fusion.2.coarse_mine), channel_id=1, source_target_pairs={{0,128},{128,0},{1,129},{129,1},{2,130},{130,2},{3,131},{131,3},{4... | collective-permute-start | bytes 491528 | tf_op jit(solution)/shard_map/ppermute | solution.py:260
  30.4 6.8 %collective-permute-start.5 = (bf16[2,784,128]{2,1,0:T(8,128)(2,1)}, bf16[2,784,128]{2,1,0:T(8,128)(2,1)S(1)}, u32[]{:S(2)}, u32[]{:S(2)}) collective-permute-start(bf16[2,784,128]{2,1,0:T(8,128)(2,1)} %collective-permute-done.3.refs_0_), channel_id=1, source_target_pairs={{0,8},{8,0},{1,9},{9,1},{2,10},{10,2},{3,11},{11,3},{4,12},{12,4},... | collective-permute-start | bytes 1204232 | tf_op jit(solution)/shard_map/ppermute | solution.py:260
  30.4 6.8 %collective-permute-start.6 = (bf16[2,784,128]{2,1,0:T(8,128)(2,1)}, bf16[2,784,128]{2,1,0:T(8,128)(2,1)S(1)}, u32[]{:S(2)}, u32[]{:S(2)}) collective-permute-start(bf16[2,784,128]{2,1,0:T(8,128)(2,1)} %collective-permute-done.4.refs_2_), channel_id=1, source_target_pairs={{0,8},{8,0},{1,9},{9,1},{2,10},{10,2},{3,11},{11,3},{4,12},{12,4},... | collective-permute-start | bytes 1204232 | tf_op jit(solution)/shard_map/ppermute | solution.py:260
  30.9 18.1 %collective-permute-start.7 = (bf16[2,784,128]{2,1,0:T(8,128)(2,1)}, bf16[2,784,128]{2,1,0:T(8,128)(2,1)S(1)}, u32[]{:S(2)}, u32[]{:S(2)}) collective-permute-start(bf16[2,784,128]{2,1,0:T(8,128)(2,1)} %collective-permute-done.3.refs_0_), channel_id=1, source_target_pairs={{0,32},{8,104},{16,48},{24,120},{32,64},{40,8},{48,80},{56,24},{64... | collective-permute-start | bytes 1204232 | tf_op jit(solution)/shard_map/ppermute | solution.py:269
  32.3 16.7 %collective-permute-start.8 = (bf16[1,784,128]{2,1,0:T(8,128)(2,1)S(1)}, bf16[1,784,128]{2,1,0:T(8,128)(2,1)S(1)}, u32[]{:S(2)}, u32[]{:S(2)}) collective-permute-start(bf16[1,784,128]{2,1,0:T(8,128)(2,1)S(1)} %slice.27), channel_id=1, source_target_pairs={{0,32},{8,104},{16,48},{24,120},{32,64},{40,8},{48,80},{56,24},{64... | collective-permute-start | bytes 602120 | tf_op jit(solution)/shard_map/ppermute | solution.py:269
  49.0 2.1 %collective-permute-start.9 = (bf16[2,784,128]{2,1,0:T(8,128)(2,1)S(1)}, bf16[2,784,128]{2,1,0:T(8,128)(2,1)S(1)}, u32[]{:S(2)}, u32[]{:S(2)}) collective-permute-start(bf16[2,784,128]{2,1,0:T(8,128)(2,1)S(1)} %collective-permute-done.7.refs_0_), channel_id=1, source_target_pairs={{0,8},{8,0},{1,9},{9,1},{2,10},{10,2},{3,11},{11,3},{4,12},{12,4},... | collective-permute-start | bytes 1204232 | tf_op jit(solution)/shard_map/ppermute | solution.py:260
  49.1 2.0 %collective-permute-start.10 = (bf16[1,784,128]{2,1,0:T(8,128)(2,1)S(1)}, bf16[1,784,128]{2,1,0:T(8,128)(2,1)S(1)}, u32[]{:S(2)}, u32[]{:S(2)}) collective-permute-start(bf16[1,784,128]{2,1,0:T(8,128)(2,1)S(1)} %collective-permute-done.8.refs_2_), channel_id=1, source_target_pairs={{0,8},{8,0},{1,9},{9,1},{2,10},{10,2},{3,11},{11,3},{4,12},{12,4},... | collective-permute-start | bytes 602120 | tf_op jit(solution)/shard_map/ppermute | solution.py:260
  55.7 13.4 %collective-permute-start.11 = (bf16[192,640]{1,0:T(8,128)(2,1)S(1)}, bf16[192,640]{1,0:T(8,128)(2,1)S(1)}, u32[]{:S(2)}, u32[]{:S(2)}) collective-permute-start(bf16[192,640]{1,0:T(8,128)(2,1)S(1)} %get-tuple-element.59), channel_id=1, source_target_pairs={{0,128},{128,0},{1,129},{129,1},{2,130},{130,2},{3,131},{131,3},{4... | collective-permute-start | bytes 737288 | tf_op jit(solution)/shard_map/ppermute | solution.py:260
  56.2 12.8 %collective-permute-start.13 = (bf16[192,640]{1,0:T(8,128)(2,1)S(1)}, bf16[192,640]{1,0:T(8,128)(2,1)S(1)}, u32[]{:S(2)}, u32[]{:S(2)}) collective-permute-start(bf16[192,640]{1,0:T(8,128)(2,1)S(1)} %get-tuple-element.61), channel_id=1, source_target_pairs={{0,130},{2,128},{128,2},{130,0},{1,131},{3,129},{129,3},{131,1},{4... | collective-permute-start | bytes 737288 | tf_op jit(solution)/shard_map/ppermute | solution.py:260
  62.3 9.5 %collective-permute-start.12 = (bf16[192,640]{1,0:T(8,128)(2,1)S(1)}, bf16[192,640]{1,0:T(8,128)(2,1)S(1)}, u32[]{:S(2)}, u32[]{:S(2)}) collective-permute-start(bf16[192,640]{1,0:T(8,128)(2,1)S(1)} %get-tuple-element.60), channel_id=1, source_target_pairs={{0,2},{2,0},{1,3},{3,1},{4,6},{6,4},{5,7},{7,5},{8,10},{10,8},{9,1... | collective-permute-start | bytes 737288 | tf_op jit(solution)/shard_map/ppermute | solution.py:260
  71.8 6.5 %collective-permute-start.15 = (bf16[256,4096]{1,0:T(8,128)(2,1)S(1)}, bf16[256,4096]{1,0:T(8,128)(2,1)}, u32[]{:S(2)}, u32[]{:S(2)}) collective-permute-start(bf16[256,4096]{1,0:T(8,128)(2,1)S(1)} %after.1.w_mine), channel_id=1, source_target_pairs={{0,8},{8,0},{1,9},{9,1},{2,10},{10,2},{3,11},{11,3},{4,12},{12,4},... | collective-permute-start | bytes 6291464 | tf_op jit(solution)/shard_map/ppermute | solution.py:260
  71.8 2.2 %copy-start = (bf16[512,4096]{1,0:T(8,128)(2,1)S(1)}, bf16[512,4096]{1,0:T(8,128)(2,1)}, u32[]{:S(2)}) copy-start(bf16[512,4096]{1,0:T(8,128)(2,1)} %w.1) | copy-start | bytes 12582916
  81.5 12.0 %collective-permute-start.16 = (bf16[48,4096]{1,0:T(8,128)(2,1)S(1)}, bf16[48,4096]{1,0:T(8,128)(2,1)S(1)}, u32[]{:S(2)}, u32[]{:S(2)}) collective-permute-start(bf16[48,4096]{1,0:T(8,128)(2,1)S(1)} %get-tuple-element.65), channel_id=1, source_target_pairs={{0,1},{1,0},{2,3},{3,2},{4,5},{5,4},{6,7},{7,6},{8,9},{9,8},{10,11... | collective-permute-start | bytes 1179656 | tf_op jit(solution)/shard_map/ppermute | solution.py:260
  82.6 20.1 %collective-permute-start.17 = (bf16[48,4096]{1,0:T(8,128)(2,1)S(1)}, bf16[48,4096]{1,0:T(8,128)(2,1)S(1)}, u32[]{:S(2)}, u32[]{:S(2)}) collective-permute-start(bf16[48,4096]{1,0:T(8,128)(2,1)S(1)} %get-tuple-element.66), channel_id=1, source_target_pairs={{0,4},{4,0},{1,5},{5,1},{2,6},{6,2},{3,7},{7,3},{8,12},{12,8},{9,1... | collective-permute-start | bytes 1179656 | tf_op jit(solution)/shard_map/ppermute | solution.py:260
  85.5 18.3 %collective-permute-start.18 = (bf16[48,4096]{1,0:T(8,128)(2,1)S(1)}, bf16[48,4096]{1,0:T(8,128)(2,1)S(1)}, u32[]{:S(2)}, u32[]{:S(2)}) collective-permute-start(bf16[48,4096]{1,0:T(8,128)(2,1)S(1)} %get-tuple-element.67), channel_id=1, source_target_pairs={{0,5},{1,4},{4,1},{5,0},{2,7},{3,6},{6,3},{7,2},{8,13},{9,12},{12,... | collective-permute-start | bytes 1179656 | tf_op jit(solution)/shard_map/ppermute | solution.py:260
